TPU v7x, 32 devices: a whole 2x2x4 slice. The times are simulated.
32 devices in a mesh: req: 4 (over z), exp: 8 (over y, x, core).
Axes of the slice: x: 2, y: 2, z: 4, core: 2. Of those that a mesh axis runs over, the one named last changes fastest.
Arguments:
- queries: bfloat16 [64, 32, 2304], P(('req', 'exp')), may hold values from -8 to 8
- draft_keys: bfloat16 [64, 32, 2304], P(('req', 'exp')), may hold values from -9 to 9
- draft_values: bfloat16 [64, 32, 2304], P(('req', 'exp')), may hold values from -6 to 6
- tree_parents: int32 [64, 32], P(('req', 'exp')), may hold values from -1 to 30, as said below
- cache_keys: bfloat16 [64, 768, 2304], P(('req', 'exp')), may hold values from -9 to 9
- cache_values: bfloat16 [64, 768, 2304], P(('req', 'exp')), may hold values from -6 to 6
- cache_lengths: int32 [64], P(('req', 'exp')), may hold values from 1 to 768, as said below
- prompt_keys: bfloat16 [8, 512, 2304], P('req', 'exp'), may hold values from -9 to 9
- prompt_values: bfloat16 [8, 512, 2304], P('req', 'exp'), may hold values from -6 to 6
- group_ids: int32 [64], P(('req', 'exp')), may hold values from 0 to 1
- residual: bfloat16 [64, 32, 2304], P(('req', 'exp')), may hold values from -6 to 6
- norm_gain: float32 [2304], replicated, may hold values from 0.5 to 1.5
- router: bfloat16 [2304, 8], replicated, may hold values from -0.125 to 0.125
- w_gate: bfloat16 [8, 2304, 5760], P('exp', None, 'req'), may hold values from -0.125 to 0.125
- w_up: bfloat16 [8, 2304, 5760], P('exp', None, 'req'), may hold values from -0.125 to 0.125
- w_down: bfloat16 [8, 5760, 2304], P('exp', 'req'), may hold values from -0.078125 to 0.078125
- expert_ids: int32 [64, 32, 2], P(('req', 'exp')), may hold values from 0 to 7, all different within a row; in each aligned block of 64 rows (0 to 63, 64 to 127, ..., all dimensions but the last counted through in order) at most 18 rows name the same one
- accepted_rows: int32 [64, 8], P(('req', 'exp')), may hold values from 0 to 31
Outputs:
- attended: bfloat16 [64, 32, 2304], P(('req', 'exp'))
- layer_out: bfloat16 [64, 32, 2304], P(('req', 'exp'))
- accepted_cache: bfloat16 [64, 2, 8, 2304], P(('req', 'exp'))
Inputs may be any that keep to these rules, and one draw needn't show every extreme that they name: `tree_parents`: position 0 of every tree holds -1; every other position holds an earlier position of the same tree. `cache_lengths`: some request has all 768 slots used. `expert_ids`: the two experts of a position differ; among the rows of one device no expert is named more than 18 times, a bound that some block reaches.
All inputs are finite; a program needn't handle non-finite values.
Results may differ from a plain program's by a relative error of at most 0.013.
Values may be sent and summed in bfloat16 or wider, within the bound.
A program may use at most 192 MiB of HBM per device.

v0:
```python
import jax
import jax.numpy as jnp
from jax import lax
from jax.sharding import PartitionSpec as P

HEADS = 36
HDIM = 64
EXPERTS = 8
TOPK = 2
GRP = 2
CAP = 18


HIGH = lax.Precision.HIGHEST
EPSILON = 1e-05


def ancestry(parents):
    length = parents.shape[-1]
    column = jnp.arange(length, dtype=jnp.int32)
    reached = (parents[..., :, None] == column).astype(jnp.float32) + jnp.eye(
        length, dtype=jnp.float32
    )
    for repeat in range(max(1, (length - 1).bit_length())):
        reached = (jnp.einsum("...ij,...jk->...ik", reached, reached, precision=HIGH) > 0.5).astype(
            jnp.float32
        )
    return reached > 0.5


def slot_numbers(picked_ids):
    flattened = picked_ids.reshape(-1)
    onehot = (flattened[:, None] == jnp.arange(EXPERTS, dtype=jnp.int32)[None, :]).astype(jnp.int32)
    before = jnp.cumsum(onehot, axis=0) - onehot
    return jnp.sum(before * onehot, axis=1).reshape(picked_ids.shape)


def on_device(
    queries,
    draft_keys,
    draft_values,
    tree_parents,
    cache_keys,
    cache_values,
    cache_lengths,
    prompt_keys,
    prompt_values,
    group_ids,
    residual,
    norm_gain,
    router,
    w_gate,
    w_up,
    w_down,
    expert_ids,
    accepted_rows,
):
    requests, tree_len, width = queries.shape
    row_count = requests * tree_len
    score_scale = HDIM ** (-0.5)
    heads_q = queries.reshape(requests, tree_len, HEADS, HDIM)
    cache_heads = cache_keys.reshape(requests, -1, HEADS, HDIM)
    cache_vals = cache_values.reshape(requests, -1, HEADS, HDIM)
    cache_scores = (
        jnp.einsum("bthd,bchd->bthc", heads_q, cache_heads, preferred_element_type=jnp.float32)
        * score_scale
    )
    live_cache = jnp.arange(cache_heads.shape[1], dtype=jnp.int32)[None, :] < cache_lengths[:, None]
    cache_scores = jnp.where(live_cache[:, None, None, :], cache_scores, -jnp.inf)
    draft_heads = draft_keys.reshape(requests, tree_len, HEADS, HDIM)
    draft_vals = draft_values.reshape(requests, tree_len, HEADS, HDIM)
    tree_scores = (
        jnp.einsum("bthd,bshd->bths", heads_q, draft_heads, preferred_element_type=jnp.float32)
        * score_scale
    )
    tree_scores = jnp.where(ancestry(tree_parents)[:, :, None, :], tree_scores, -jnp.inf)
    local_top = jnp.maximum(jnp.max(cache_scores, axis=-1), jnp.max(tree_scores, axis=-1))
    cache_weights = jnp.exp(cache_scores - local_top[..., None])
    tree_weights = jnp.exp(tree_scores - local_top[..., None])
    local_total = jnp.sum(cache_weights, axis=-1) + jnp.sum(tree_weights, axis=-1)
    local_acc = jnp.einsum(
        "bthc,bchd->bthd",
        cache_weights.astype(jnp.bfloat16),
        cache_vals,
        preferred_element_type=jnp.float32,
    )
    local_acc = local_acc + jnp.einsum(
        "bths,bshd->bthd",
        tree_weights.astype(jnp.bfloat16),
        draft_vals,
        preferred_element_type=jnp.float32,
    )
    local_top = local_top.reshape(row_count, HEADS)
    local_total = local_total.reshape(row_count, HEADS)
    local_acc = local_acc.reshape(row_count, HEADS, HDIM)
    member = jnp.repeat(group_ids, tree_len)[:, None] == jnp.arange(GRP, dtype=jnp.int32)[None, :]
    query_rows = heads_q.reshape(row_count, HEADS, HDIM)
    running_top = local_top
    summed = local_total
    gathered_acc = local_acc
    key_piece = lax.all_gather(prompt_keys, "exp", axis=1, tiled=True)
    value_piece = lax.all_gather(prompt_values, "exp", axis=1, tiled=True)
    key_count = key_piece.shape[1]
    key_heads = key_piece.reshape(GRP, key_count, HEADS, HDIM)
    value_heads = value_piece.reshape(GRP, key_count, HEADS, HDIM)
    block_scores = (
        jnp.einsum("rhd,gkhd->rhgk", query_rows, key_heads, preferred_element_type=jnp.float32)
        * score_scale
    )
    block_scores = jnp.where(member[:, None, :, None], block_scores, -jnp.inf)
    new_top = jnp.maximum(running_top, jnp.max(block_scores, axis=(2, 3)))
    shrink = jnp.exp(running_top - new_top)
    block_weights = jnp.exp(block_scores - new_top[:, :, None, None])
    summed = summed * shrink + jnp.sum(block_weights, axis=(2, 3))
    gathered_acc = gathered_acc * shrink[:, :, None] + jnp.einsum(
        "rhgk,gkhd->rhd",
        block_weights.astype(jnp.bfloat16),
        value_heads,
        preferred_element_type=jnp.float32,
    )
    running_top, summed, gathered_acc = (new_top, summed, gathered_acc)
    attended = (
        (gathered_acc / summed[:, :, None]).reshape(requests, tree_len, width).astype(jnp.bfloat16)
    )
    stream = (residual.astype(jnp.float32) + attended.astype(jnp.float32)).astype(jnp.bfloat16)
    stream_rows = stream.reshape(row_count, width).astype(jnp.float32)
    normed = (
        stream_rows
        * lax.rsqrt(jnp.mean(stream_rows * stream_rows, axis=-1, keepdims=True) + EPSILON)
        * norm_gain
    ).astype(jnp.bfloat16)
    logits = jnp.dot(normed, router, preferred_element_type=jnp.float32)
    routed = expert_ids.reshape(row_count, TOPK)
    chosen = jnp.take_along_axis(logits, routed, axis=1)
    gate_first = 1.0 / (1.0 + jnp.exp(chosen[:, 1] - chosen[:, 0]))
    gates = jnp.stack([gate_first, 1.0 - gate_first], axis=1)
    target = routed * CAP + slot_numbers(routed)
    buffer = (
        jnp.zeros((EXPERTS * CAP, width), jnp.bfloat16)
        .at[target.reshape(-1)]
        .set(jnp.repeat(normed, TOPK, axis=0))
    )
    holder_count = lax.axis_size("exp")
    holders = holder_count // EXPERTS
    outgoing = jnp.broadcast_to(
        buffer.reshape(EXPERTS, 1, CAP, width), (EXPERTS, holders, CAP, width)
    ).reshape(holder_count, CAP, width)
    gate_local = w_gate[0]
    up_local = w_up[0]
    down_local = w_down[0]
    arrived = lax.all_to_all(outgoing, "exp", split_axis=0, concat_axis=0, tiled=True)
    row_piece = lax.all_gather(arrived.reshape(-1, width), "req", axis=0, tiled=True)
    gate_proj = jnp.dot(row_piece, gate_local, preferred_element_type=jnp.float32)
    up_proj = jnp.dot(row_piece, up_local, preferred_element_type=jnp.float32)
    hidden = (jax.nn.silu(gate_proj) * up_proj).astype(jnp.bfloat16)
    summed_rows = lax.psum_scatter(
        jnp.dot(hidden, down_local, preferred_element_type=jnp.float32).astype(jnp.bfloat16),
        "req",
        scatter_dimension=0,
        tiled=True,
    )
    returned = lax.all_to_all(
        summed_rows.reshape(holder_count, CAP, width),
        "exp",
        split_axis=0,
        concat_axis=0,
        tiled=True,
    )
    expert_result = (
        returned.astype(jnp.float32)
        .reshape(EXPERTS, holders, CAP, width)
        .sum(axis=1)
        .reshape(EXPERTS * CAP, width)
    )
    picked = expert_result[target]
    layer_out = (
        (stream_rows + jnp.sum(gates[:, :, None] * picked, axis=1))
        .astype(jnp.bfloat16)
        .reshape(requests, tree_len, width)
    )
    kept_keys = jnp.take_along_axis(draft_keys, accepted_rows[:, :, None], axis=1)
    kept_values = jnp.take_along_axis(draft_values, accepted_rows[:, :, None], axis=1)
    accepted_cache = jnp.stack([kept_keys, kept_values], axis=1)
    return (attended, layer_out, accepted_cache)


def solution(mesh):
    return jax.shard_map(
        on_device,
        mesh=mesh,
        in_specs=(
            P(("req", "exp"), None, None),
            P(("req", "exp"), None, None),
            P(("req", "exp"), None, None),
            P(("req", "exp"), None),
            P(("req", "exp"), None, None),
            P(("req", "exp"), None, None),
            P(("req", "exp")),
            P("req", "exp", None),
            P("req", "exp", None),
            P(("req", "exp")),
            P(("req", "exp"), None, None),
            P(),
            P(),
            P("exp", None, "req"),
            P("exp", None, "req"),
            P("exp", "req", None),
            P(("req", "exp"), None, None),
            P(("req", "exp"), None),
        ),
        out_specs=(
            P(("req", "exp"), None, None),
            P(("req", "exp"), None, None),
            P(("req", "exp"), None, None, None),
        ),
        check_vma=False,
    )
```

profile of v0, /device:TPU:0, one launch (start us, length us, event | category | flops | bytes accessed | tf_op | source)
XLA Modules:
  0.0 296.1 jit_solution(12981081108997633056)
XLA Ops:
  7.2 2.5 copy.75
  9.8 2.5 copy.79
  13.8 2.5 reshape_reshape.6
  16.4 10.3 %copy.70 = bf16[2,768,2304]{1,2,0:T(8,128)(2,1)} copy(bf16[2,768,2304]{2,1,0:T(8,128)(2,1)} %param.25) | data formatting | bytes 14155776 | tf_op args[5]
  26.7 10.4 %copy.65 = bf16[2,768,2304]{1,2,0:T(8,128)(2,1)} copy(bf16[2,768,2304]{2,1,0:T(8,128)(2,1)} %param.24) | data formatting | bytes 14155776 | tf_op args[4]
  41.4 4.9 %bitcast_reduce_fusion = (f32[2,32,36]{1,2,0:T(8,128)S(1)}, f32[2,36,768,32]{2,3,1,0:T(8,128)S(1)}) fusion(pred[2,768]{1,0:T(4,128)(4,1)S(1)} %iota_compare_fusion.4, bf16[2,768,36,64]{1,3,2,0:T(8,128)(2,1)} %bitcast.124, bf16[2,32,36,64]{3,2,1,0:T(8,128)(2,1)} %copy-done.10), kind=kOutput, calls=%fused_computation.11 | convolution fusion | flops 231798528 | bytes 14461440 | tf_op jit(solution)/shard_map/bthd,bchd->bthc/dot_general | solution.py:65
  46.4 3.3 %fusion.24 = f32[2,36,32,64]{3,2,1,0:T(8,128)} fusion(bf16[2,768,36,64]{1,3,2,0:T(8,128)(2,1)S(1)} %bitcast.128, f32[2,36,768,32]{2,3,1,0:T(8,128)S(1)} %get-tuple-element.15, f32[2,32,36]{1,2,0:T(8,128)S(1)} %max.36, pred[2,768]{1,0:T(4,128)(4,1)S(1)} %iota_compare_fusion.4), kind=kOutput, calls=%fused_computation.31 | convolution fusion | flops 233570304 | bytes 14756352 | tf_op jit(solution)/shard_map/bthc,bchd->bthd/dot_general | solution.py:81
  49.7 2.4 fusion.37
  52.9 4.0 %fusion.10 = f32[2,32,36]{1,2,0:T(8,128)S(1)} fusion(f32[2,36,768,32]{2,3,1,0:T(8,128)} %copy-done.2, f32[2,32,36]{1,2,0:T(8,128)S(1)} %max.36, pred[2,768]{1,0:T(4,128)(4,1)S(1)} %iota_compare_fusion.4), kind=kLoop, calls=%fused_computation.20 | loop fusion | flops 7075584 | bytes 7097856 | tf_op jit(solution)/shard_map/reduce_sum | solution.py:80
  58.0 12.5 %copy.76 = bf16[2,512,2304]{1,2,0:T(8,128)(2,1)} copy(bf16[2,512,2304]{2,0,1:T(2,128)(2,1)} %all-gather.4.cloned.1.call-done) | data formatting | bytes 9437184 | tf_op jit(solution)/shard_map/all_gather | solution.py:101
  70.5 3.4 %fusion.2 = (f32[64,36]{0,1:T(8,128)S(1)}, f32[36,2,512,64]{2,3,1,0:T(8,128)S(1)}) fusion(pred[64,2]{0,1:T(4,128)(4,1)S(1)} %iota_compare_fusion.5, bf16[2,512,36,64]{1,3,2,0:T(8,128)(2,1)} %bitcast.125, bf16[64,36,64,1]{2,1,0,3:T(8,128)(2,1)S(1)} %bitcast.130), kind=kOutput, calls=%fused_computation.9 | convolution fusion | flops 309065472 | bytes 14460032 | tf_op jit(solution)/shard_map/rhd,gkhd->rhgk/dot_general | solution.py:107
  73.9 2.3 fusion
  78.1 14.3 %all-gather.6.cloned.1.call-done = bf16[2,512,2304]{2,0,1:T(2,128)(2,1)} async-done(((bf16[2,64,2304]{2,0,1:T(2,128)(2,1)}), bf16[2,512,2304]{2,0,1:T(2,128)(2,1)}) %all-gather.6.cloned.1.call-update) | async-done | bytes 4718608 | tf_op jit(solution)/shard_map/all_gather | solution.py:102
  92.4 12.4 %copy.80 = bf16[2,512,2304]{1,2,0:T(8,128)(2,1)} copy(bf16[2,512,2304]{2,0,1:T(2,128)(2,1)} %all-gather.6.cloned.1.call-done) | data formatting | bytes 9437184 | tf_op jit(solution)/shard_map/all_gather | solution.py:102
  104.8 7.3 %divide_convert_fusion = bf16[64,36,64]{2,0,1:T(8,128)(2,1)S(1)} fusion(f32[64,36,64]{2,0,1:T(8,128)S(1)} %bitcast_multiply_fusion, bf16[2,512,36,64]{1,3,2,0:T(8,128)(2,1)} %bitcast.129, f32[36,2,512,64]{2,3,1,0:T(8,128)} %copy-done.1, f32[64,36]{0,1:T(8,128)S(1)} %max.38, pred[64,2]{0,1:T(4,128)(4,1)S(1)} %iota_compare_fusion.5, ...), kind=kOutput, calls=%fused_computation.46 | convolution fusion | flops 311869440 | bytes 15059072 | tf_op jit(solution)/shard_map/rhgk,gkhd->rhd/dot_general | solution.py:115
  115.7 16.2 %all_to_all.10 = bf16[8,18,2304]{2,1,0:T(8,128)(2,1)S(1)} all-to-all(bf16[8,18,2304]{2,1,0:T(8,128)(2,1)S(1)} %reshape_reshape.7), channel_id=1, replica_groups=mesh['req'=4,'exp'=8] {'exp'}, dimensions={0} | all-to-all | bytes 1327104 | tf_op jit(solution)/shard_map/all_to_all | solution.py:151
  133.0 54.6 %all-gather.8.cloned.1.call-done = bf16[576,2304]{1,0:T(8,128)(2,1)} async-done(((bf16[144,2304]{1,0:T(8,128)(2,1)}), bf16[576,2304]{1,0:T(8,128)(2,1)}) %all-gather.8.cloned.1.call-update) | async-done | bytes 2654224 | tf_op jit(solution)/shard_map/all_gather | solution.py:152
  187.6 9.7 %fusion.8 = f32[576,1440]{1,0:T(8,128)} fusion(bf16[576,2304]{1,0:T(8,128)(2,1)} %all-gather.8.cloned.1.call-done, bf16[1,2304,1440]{1,2,0:T(8,128)(2,1)} %param.33), kind=kOutput, calls=%fused_computation.18 | convolution fusion | flops 3822059520 | bytes 12607488 | tf_op jit(solution)/shard_map/dot_general | solution.py:153
  197.3 16.7 %fusion.21 = bf16[576,2304]{1,0:T(8,128)(2,1)} fusion(bf16[1,1440,2304]{2,1,0:T(8,128)(2,1)} %param.35, f32[576,1440]{1,0:T(8,128)} %fusion.8, bf16[576,2304]{1,0:T(8,128)(2,1)} %all-gather.8.cloned.1.call-done, bf16[1,2304,1440]{1,2,0:T(8,128)(2,1)} %param.34), kind=kOutput, calls=%fused_computation.30 | convolution fusion | flops 7650422784 | bytes 21897216 | tf_op jit(solution)/shard_map/dot_general | solution.py:157
  217.4 48.2 %reduce-scatter.2.cloned.1.call-done = bf16[144,2304]{1,0:T(8,128)(2,1)} async-done(((bf16[576,2304]{1,0:T(8,128)(2,1)}), bf16[144,2304]{1,0:T(8,128)(2,1)}) %reduce-scatter.2.cloned.1.call-update) | async-done | bytes 663568 | tf_op jit(solution)/shard_map/reduce_scatter | solution.py:156
  265.6 2.2 reshape.302
  267.8 3.8 %all-to-all-start.1 = ((bf16[8,18,2304]{2,1,0:T(8,128)(2,1)}), bf16[8,18,2304]{2,1,0:T(8,128)(2,1)S(1)}, u32[]{:S(2)}, u32[]{:S(2)}) async-start(bf16[8,18,2304]{2,1,0:T(8,128)(2,1)} %reshape.302), calls=%async_computation.2 | async-start | bytes 1769472 | tf_op jit(solution)/shard_map/all_to_all | solution.py:162
  273.2 11.9 %all-to-all-done.1 = bf16[8,18,2304]{2,1,0:T(8,128)(2,1)S(1)} async-done(((bf16[8,18,2304]{2,1,0:T(8,128)(2,1)}), bf16[8,18,2304]{2,1,0:T(8,128)(2,1)S(1)}, u32[]{:S(2)}, u32[]{:S(2)}) %all-to-all-start.1) | async-done | bytes 663584 | tf_op jit(solution)/shard_map/all_to_all | solution.py:162
  287.1 1.6 multiply_reduce_fusion
  (132 shorter events, 22.0 us)
Async XLA Ops:
  7.2 264.4 %copy-start = (bf16[2304,8]{0,1:T(8,128)(2,1)S(1)}, bf16[2304,8]{0,1:T(8,128)(2,1)}, u32[]{:S(2)}) copy-start(bf16[2304,8]{0,1:T(8,128)(2,1)} %param.32) | copy-start | bytes 110596
  7.2 50.8 %all-gather.4.cloned.1.call-start = ((), (), s32[]{:S(2)}) async-start(), calls=%async_computation.3 | async-start | bytes 5308416 | tf_op jit(solution)/shard_map/all_gather | solution.py:101
  9.8 82.6 %all-gather.6.cloned.1.call-start = ((), (), s32[]{:S(2)}) async-start(), calls=%async_computation.4 | async-start | bytes 5308416 | tf_op jit(solution)/shard_map/all_gather | solution.py:102
  12.3 175.2 %all-gather.8.cloned.1.call-start = ((), (), s32[]{:S(2)}) async-start(), calls=%async_computation.5 | async-start | bytes 3317760 | tf_op jit(solution)/shard_map/all_gather | solution.py:152
  13.8 26.2 %copy-start.10 = (bf16[2,32,36,64]{3,2,1,0:T(8,128)(2,1)}, bf16[2,32,36,64]{3,2,1,0:T(8,128)(2,1)S(1)}, u32[]{:S(2)}) copy-start(bf16[2,32,36,64]{3,2,1,0:T(8,128)(2,1)S(1)} %reshape.291) | copy-start | bytes 884740
  26.7 10.4 %copy-start.4 = (bf16[2,32,2304]{2,1,0:T(8,128)(2,1)S(1)}, bf16[2,32,2304]{2,1,0:T(8,128)(2,1)}, u32[]{:S(2)}) copy-start(bf16[2,32,2304]{2,1,0:T(8,128)(2,1)} %param.21) | copy-start | bytes 884740
  26.7 10.9 %copy-start.17 = (s32[2,32]{1,0:T(2,128)S(1)}, s32[2,32]{1,0:T(2,128)}, u32[]{:S(2)}) copy-start(s32[2,32]{1,0:T(2,128)} %param.23) | copy-start | bytes 772
  26.7 11.9 %copy-start.5 = (bf16[2,32,2304]{2,1,0:T(8,128)(2,1)S(1)}, bf16[2,32,2304]{2,1,0:T(8,128)(2,1)}, u32[]{:S(2)}) copy-start(bf16[2,32,2304]{2,1,0:T(8,128)(2,1)} %param.22) | copy-start | bytes 884740
  26.7 13.2 %copy-start.16 = (s32[2]{0:T(128)S(1)}, s32[2]{0:T(128)}, u32[]{:S(2)}) copy-start(s32[2]{0:T(128)} %param.26) | copy-start | bytes 28
  40.0 6.4 %slice-start = ((s8[7077888]{0:T(1024)(128)(4,1)}), s8[4194304]{0:T(1024)(128)(4,1)S(1)}, s32[]{:S(2)}) async-start(s8[7077888]{0:T(1024)(128)(4,1)} %bitcast.126), calls=%async_computation.7 | async-start | bytes 8388608
  41.4 5.0 %slice-start.1 = ((s8[7077888]{0:T(1024)(128)(4,1)}), s8[2883584]{0:T(1024)(128)(4,1)S(1)}, s32[]{:S(2)}) async-start(s8[7077888]{0:T(1024)(128)(4,1)} %bitcast.126), calls=%async_computation.8 | async-start | bytes 5767168
  46.3 3.4 %copy-start.2 = (f32[2,36,768,32]{2,3,1,0:T(8,128)}, f32[2,36,768,32]{2,3,1,0:T(8,128)S(1)}, u32[]{:S(2)}) copy-start(f32[2,36,768,32]{2,3,1,0:T(8,128)S(1)} %get-tuple-element.15) | copy-start | bytes 21233668
  49.7 2.8 copy-start.3
  52.3 4.7 %copy-start.13 = (s32[2,32,2]{1,2,0:T(2,128)S(1)}, s32[2,32,2]{1,2,0:T(2,128)}, u32[]{:S(2)}) copy-start(s32[2,32,2]{1,2,0:T(2,128)} %param.36) | copy-start | bytes 1540
  57.9 12.5 %copy-start.9 = (bf16[64,36,64]{2,1,0:T(8,128)(2,1)S(1)}, bf16[64,36,64]{2,1,0:T(8,128)(2,1)}, u32[]{:S(2)}) copy-start(bf16[64,36,64]{2,1,0:T(8,128)(2,1)} %reshape_reshape.6) | copy-start | bytes 884740
  73.8 3.9 %copy-start.1 = (f32[36,2,512,64]{2,3,1,0:T(8,128)}, f32[36,2,512,64]{2,3,1,0:T(8,128)S(1)}, u32[]{:S(2)}) copy-start(f32[36,2,512,64]{2,3,1,0:T(8,128)S(1)} %get-tuple-element.19) | copy-start | bytes 28311556
  104.8 8.1 %copy-start.11 = (bf16[2,32,2304]{2,1,0:T(8,128)(2,1)S(1)}, bf16[2,32,2304]{2,1,0:T(8,128)(2,1)}, u32[]{:S(2)}) copy-start(bf16[2,32,2304]{2,1,0:T(8,128)(2,1)} %param.30) | copy-start | bytes 884740
  104.8 8.5 %copy-start.14 = (f32[2304]{0:T(1024)S(1)}, f32[2304]{0:T(1024)}, u32[]{:S(2)}) copy-start(f32[2304]{0:T(1024)} %param.31) | copy-start | bytes 27652
  133.0 132.6 %reduce-scatter.2.cloned.1.call-start = ((), (), s32[]{:S(2)}) async-start(), calls=%async_computation.6 | async-start | bytes 3317760 | tf_op jit(solution)/shard_map/reduce_scatter | solution.py:156
  197.3 17.0 %copy-start.15 = (s32[2,8]{1,0:T(2,128)S(1)}, s32[2,8]{1,0:T(2,128)}, u32[]{:S(2)}) copy-start(s32[2,8]{1,0:T(2,128)} %param.37) | copy-start | bytes 196
  197.3 17.9 %copy-start.6 = (bf16[2,32,2304]{2,1,0:T(8,128)(2,1)S(1)}, bf16[2,32,2304]{2,1,0:T(8,128)(2,1)}, u32[]{:S(2)}) copy-start(bf16[2,32,2304]{2,1,0:T(8,128)(2,1)} %param.22) | copy-start | bytes 884740
  267.8 17.3 %all-to-all-start.1 = ((bf16[8,18,2304]{2,1,0:T(8,128)(2,1)}), bf16[8,18,2304]{2,1,0:T(8,128)(2,1)S(1)}, u32[]{:S(2)}, u32[]{:S(2)}) async-start(bf16[8,18,2304]{2,1,0:T(8,128)(2,1)} %reshape.302), calls=%async_computation.2 | async-start | bytes 1769472 | tf_op jit(solution)/shard_map/all_to_all | solution.py:162
  285.3 3.5 %copy-start.8 = (bf16[2,32,2304]{2,1,0:T(8,128)(2,1)S(1)}, bf16[2,32,2304]{2,1,0:T(8,128)(2,1)}, u32[]{:S(2)}) copy-start(bf16[2,32,2304]{2,1,0:T(8,128)(2,1)} %copy-done.7) | copy-start | bytes 884740
  285.3 3.5 %copy-start.12 = (bf16[2,32,2304]{2,1,0:T(8,128)(2,1)S(1)}, bf16[2,32,2304]{2,1,0:T(8,128)(2,1)}, u32[]{:S(2)}) copy-start(bf16[2,32,2304]{2,1,0:T(8,128)(2,1)} %param.30) | copy-start | bytes 884740
  (2 other events, 3.6 us)
Sparse Core Ops, SparseCore 0:
  9.9 41.6 all-gather.3
  53.4 38.9 all-gather.5
  133.1 54.4 all-gather.7
  214.2 51.3 reduce-scatter.1
where the time goes:
time: 298 us; the launch traced here: 296 us
  waiting for transfers between devices  129 us (43%)
  local copies, waits for them, and re-layouts  71.3 us (24%)
  matrix products  50.2 us (17%)
  blocking collectives  16.2 us (5%)
  between operations  14.3 us (5%)
  other arithmetic  11.3 us (4%)
  starting transfers between devices  3.93 us (1%)
    all_gather x1, waiting for transfers between devices, on_device(): lax.all_gather(arrived.reshape(-1, width), 'req', axis=0, tiled=True)  54.6 us
    reduce_scatter x1, waiting for transfers between devices, on_device(): lax.psum_scatter(jnp.dot(hidden, down_local, preferred_element_type=jnp.f...  48.2 us
    unnamed x48, local copies, waits for them, and re-layouts  27.5 us
    dot_general x1, matrix products, on_device(): jnp.dot(hidden, down_local, preferred_element_type=jnp.float32)  16.7 us
    all_to_all x1, blocking collectives, on_device(): lax.all_to_all(outgoing, 'exp', split_axis=0, concat_axis=0, tiled=True)  16.2 us
    all_gather x1, waiting for transfers between devices, on_device(): value_piece = lax.all_gather(prompt_values, 'exp', axis=1, tiled=True)  14.3 us
    all_gather x1, local copies, waits for them, and re-layouts, on_device(): key_piece = lax.all_gather(prompt_keys, 'exp', axis=1, tiled=True)  12.5 us
    all_gather x1, local copies, waits for them, and re-layouts, on_device(): value_piece = lax.all_gather(prompt_values, 'exp', axis=1, tiled=True)  12.4 us
  transfers between devices with their start and end apart: 5, of which 4 were waited for; matrix products, arithmetic and copies ran while one was open for 24% of the time, Pallas kernels for 0%

commit v1 on v0

v1 whole, which is shorter than its diff:
```python
import jax
import jax.numpy as jnp
from jax import lax
from jax.experimental import pallas as pl
from jax.experimental.pallas import tpu as pltpu
from jax.sharding import PartitionSpec as P

HEADS = 36
HDIM = 64
EXPERTS = 8
TOPK = 2
GRP = 2
CAP = 18
LANES = 256
PACK = LANES // HDIM
STAT = 128


HIGH = lax.Precision.HIGHEST
EPSILON = 1e-05


def ancestry(parents):
    length = parents.shape[-1]
    column = jnp.arange(length, dtype=jnp.int32)
    reached = (parents[..., :, None] == column).astype(jnp.float32) + jnp.eye(
        length, dtype=jnp.float32
    )
    for repeat in range(max(1, (length - 1).bit_length())):
        reached = (jnp.einsum("...ij,...jk->...ik", reached, reached, precision=HIGH) > 0.5).astype(
            jnp.float32
        )
    return reached > 0.5


def slot_numbers(picked_ids):
    flattened = picked_ids.reshape(-1)
    onehot = (flattened[:, None] == jnp.arange(EXPERTS, dtype=jnp.int32)[None, :]).astype(jnp.int32)
    before = jnp.cumsum(onehot, axis=0) - onehot
    return jnp.sum(before * onehot, axis=1).reshape(picked_ids.shape)


SCALE = HDIM ** (-0.5)
NT = (((1,), (1,)), ((), ()))


def head_masks(rows):
    head = lax.broadcasted_iota(jnp.int32, (rows, LANES), 1) // HDIM
    return [(head == h).astype(jnp.float32).astype(jnp.bfloat16) for h in range(PACK)]


def local_kernel(len_ref, q_ref, kc_ref, vc_ref, kd_ref, vd_ref, anc_ref, acc_ref, stat_ref):
    b, g = pl.program_id(0), pl.program_id(1)
    tree = q_ref.shape[1]
    q = q_ref[0]
    masks = head_masks(tree)
    stacked = jnp.concatenate([q * mask for mask in masks], axis=0)
    s_cache = lax.dot_general(stacked, kc_ref[0], NT, preferred_element_type=jnp.float32) * SCALE
    slot = lax.broadcasted_iota(jnp.int32, s_cache.shape, 1)
    s_cache = jnp.where(slot < len_ref[b], s_cache, -jnp.inf)
    s_tree = lax.dot_general(stacked, kd_ref[0], NT, preferred_element_type=jnp.float32) * SCALE
    anc = jnp.concatenate([anc_ref[0]] * PACK, axis=0)
    s_tree = jnp.where(anc > 0.5, s_tree, -jnp.inf)
    top = jnp.maximum(
        jnp.max(s_cache, axis=1, keepdims=True), jnp.max(s_tree, axis=1, keepdims=True)
    )
    w_cache = jnp.exp(s_cache - top)
    w_tree = jnp.exp(s_tree - top)
    total = jnp.sum(w_cache, axis=1, keepdims=True) + jnp.sum(w_tree, axis=1, keepdims=True)
    mixed = jnp.dot(w_cache.astype(jnp.bfloat16), vc_ref[0], preferred_element_type=jnp.float32)
    mixed += jnp.dot(w_tree.astype(jnp.bfloat16), vd_ref[0], preferred_element_type=jnp.float32)
    head = lax.broadcasted_iota(jnp.int32, (tree, LANES), 1) // HDIM
    lane = lax.broadcasted_iota(jnp.int32, (tree, STAT), 1)

    @pl.when(g == 0)
    def _():
        stat_ref[...] = jnp.zeros_like(stat_ref)

    out = jnp.zeros((tree, LANES), jnp.float32)
    stat = stat_ref[0]
    for h in range(PACK):
        rows = slice(h * tree, (h + 1) * tree)
        out = jnp.where(head == h, mixed[rows], out)
        stat = jnp.where(lane == g * PACK + h, top[rows], stat)
        stat = jnp.where(lane == STAT // 2 + g * PACK + h, total[rows], stat)
    acc_ref[0] = out
    stat_ref[0] = stat


def prompt_kernel(q_ref, group_ref, k_ref, v_ref, acc_ref, stat_ref):
    g = pl.program_id(0)
    sources, rows = q_ref.shape[0], q_ref.shape[1]
    groups, positions = k_ref.shape[0], k_ref.shape[1]
    keys = groups * positions
    k = k_ref[...].reshape(keys, LANES)
    v = v_ref[...].reshape(keys, LANES)
    masks = head_masks(keys)
    k_wide = jnp.concatenate([k * mask for mask in masks], axis=0)
    v_wide = jnp.concatenate([v * mask for mask in masks], axis=0)
    key_group = (lax.broadcasted_iota(jnp.int32, (rows, keys), 1) // positions).astype(jnp.float32)
    lane = lax.broadcasted_iota(jnp.int32, (rows, STAT), 1)

    @pl.when(g == 0)
    def _():
        stat_ref[...] = jnp.zeros_like(stat_ref)

    for s in range(sources):
        scores = lax.dot_general(q_ref[s], k_wide, NT, preferred_element_type=jnp.float32) * SCALE
        live = key_group == group_ref[s].astype(jnp.float32)[:, :1]
        stat = stat_ref[s]
        weights = []
        for h in range(PACK):
            part = jnp.where(live, scores[:, h * keys : (h + 1) * keys], -jnp.inf)
            top = jnp.max(part, axis=1, keepdims=True)
            weight = jnp.exp(part - top)
            stat = jnp.where(lane == g * PACK + h, top, stat)
            stat = jnp.where(
                lane == STAT // 2 + g * PACK + h, jnp.sum(weight, axis=1, keepdims=True), stat
            )
            weights.append(weight.astype(jnp.bfloat16))
        stat_ref[s] = stat
        acc_ref[s] = jnp.dot(
            jnp.concatenate(weights, axis=1), v_wide, preferred_element_type=jnp.float32
        ).astype(jnp.bfloat16)


def merge_kernel(
    part_ref, pstat_ref, acc_ref, stat_ref, residual_ref, gain_ref, att_ref, stream_ref, normed_ref
):
    sources, rows, width = part_ref.shape
    stats = [stat_ref[...]] + [pstat_ref[s] for s in range(sources)]
    top = stats[0]
    for stat in stats[1:]:
        top = jnp.maximum(top, stat)
    scales = [jnp.exp(stat - top) for stat in stats]
    total = sum(scale * pltpu.roll(stat, STAT // 2, 1) for scale, stat in zip(scales, stats))
    scales = [scale / total for scale in scales]
    squares = jnp.zeros((rows, 1), jnp.float32)
    left = lax.broadcasted_iota(jnp.int32, (rows, STAT), 1) < HDIM
    for pair in range(width // STAT):
        cols = slice(pair * STAT, (pair + 1) * STAT)
        a = 2 * pair
        out = jnp.zeros((rows, STAT), jnp.float32)
        for i in range(sources + 1):
            values = acc_ref[:, cols] if i == 0 else part_ref[i - 1, :, cols].astype(jnp.float32)
            out += values * jnp.where(left, scales[i][:, a : a + 1], scales[i][:, a + 1 : a + 2])
        attended = out.astype(jnp.bfloat16)
        att_ref[:, cols] = attended
        stream = (
            residual_ref[:, cols].astype(jnp.float32) + attended.astype(jnp.float32)
        ).astype(jnp.bfloat16)
        stream_ref[:, cols] = stream
        stream = stream.astype(jnp.float32)
        squares += jnp.sum(stream * stream, axis=1, keepdims=True)
    factor = lax.rsqrt(squares / width + EPSILON)
    normed_ref[...] = (
        stream_ref[...].astype(jnp.float32) * factor * gain_ref[...]
    ).astype(jnp.bfloat16)


def attention(
    queries, draft_keys, draft_values, tree_parents, cache_keys, cache_values, cache_lengths,
    prompt_keys, prompt_values, group_ids, residual, norm_gain,
):
    requests, tree, width = queries.shape
    rows, packs, cache = requests * tree, width // LANES, cache_keys.shape[1]
    groups, positions = prompt_keys.shape[:2]
    row_group = jnp.broadcast_to(
        jnp.repeat(group_ids, tree)[:, None].astype(jnp.bfloat16), (rows, STAT)
    )
    sent = jnp.concatenate([queries.reshape(rows, width), row_group], axis=1)
    plane = lax.all_gather(sent, "exp", axis=0, tiled=False)
    sources = plane.shape[0]
    anc = ancestry(tree_parents).astype(jnp.float32)
    block = lambda n: pl.BlockSpec((1, n, LANES), lambda b, g, _: (b, 0, g))
    flops = 4 * rows * PACK * width * (cache + tree)
    acc, stat = pl.pallas_call(
        local_kernel,
        grid_spec=pltpu.PrefetchScalarGridSpec(
            num_scalar_prefetch=1,
            grid=(requests, packs),
            in_specs=[
                block(tree), block(cache), block(cache), block(tree), block(tree),
                pl.BlockSpec((1, tree, tree), lambda b, g, _: (b, 0, 0)),
            ],
            out_specs=[block(tree), pl.BlockSpec((1, tree, STAT), lambda b, g, _: (b, 0, 0))],
        ),
        out_shape=[
            jax.ShapeDtypeStruct((requests, tree, width), jnp.float32),
            jax.ShapeDtypeStruct((requests, tree, STAT), jnp.float32),
        ],
        cost_estimate=pl.CostEstimate(
            flops=flops, bytes_accessed=4 * requests * cache * width,
            transcendentals=rows * HEADS * cache,
        ),
        name="local_attention",
    )(cache_lengths, queries, cache_keys, cache_values, draft_keys, draft_values, anc)
    pblock = pl.BlockSpec((groups, positions, LANES), lambda g: (0, 0, g))
    part, pstat = pl.pallas_call(
        prompt_kernel,
        grid=(packs,),
        in_specs=[
            pl.BlockSpec((sources, rows, LANES), lambda g: (0, 0, g)),
            pl.BlockSpec((sources, rows, STAT), lambda g: (0, 0, width // STAT)),
            pblock,
            pblock,
        ],
        out_specs=[
            pl.BlockSpec((sources, rows, LANES), lambda g: (0, 0, g)),
            pl.BlockSpec((sources, rows, STAT), lambda g: (0, 0, 0)),
        ],
        out_shape=[
            jax.ShapeDtypeStruct((sources, rows, width), jnp.bfloat16),
            jax.ShapeDtypeStruct((sources, rows, STAT), jnp.float32),
        ],
        name="prompt_attention",
    )(plane, plane, prompt_keys, prompt_values)
    part = lax.all_to_all(part, "exp", split_axis=0, concat_axis=0, tiled=True)
    pstat = lax.all_to_all(pstat, "exp", split_axis=0, concat_axis=0, tiled=True)
    return pl.pallas_call(
        merge_kernel,
        out_shape=[jax.ShapeDtypeStruct((rows, width), jnp.bfloat16)] * 3,
        compiler_params=pltpu.CompilerParams(vmem_limit_bytes=32 * 1024 * 1024),
        name="merge",
    )(
        part, pstat, acc.reshape(rows, width), stat.reshape(rows, STAT),
        residual.reshape(rows, width), norm_gain.reshape(1, width),
    )


def on_device(
    queries,
    draft_keys,
    draft_values,
    tree_parents,
    cache_keys,
    cache_values,
    cache_lengths,
    prompt_keys,
    prompt_values,
    group_ids,
    residual,
    norm_gain,
    router,
    w_gate,
    w_up,
    w_down,
    expert_ids,
    accepted_rows,
):
    requests, tree_len, width = queries.shape
    row_count = requests * tree_len
    attended, stream, normed = attention(
        queries, draft_keys, draft_values, tree_parents, cache_keys, cache_values, cache_lengths,
        prompt_keys, prompt_values, group_ids, residual, norm_gain,
    )
    attended = attended.reshape(requests, tree_len, width)
    stream_rows = stream.astype(jnp.float32)
    logits = jnp.dot(normed, router, preferred_element_type=jnp.float32)
    routed = expert_ids.reshape(row_count, TOPK)
    chosen = jnp.take_along_axis(logits, routed, axis=1)
    gate_first = 1.0 / (1.0 + jnp.exp(chosen[:, 1] - chosen[:, 0]))
    gates = jnp.stack([gate_first, 1.0 - gate_first], axis=1)
    target = routed * CAP + slot_numbers(routed)
    buffer = (
        jnp.zeros((EXPERTS * CAP, width), jnp.bfloat16)
        .at[target.reshape(-1)]
        .set(jnp.repeat(normed, TOPK, axis=0))
    )
    holder_count = lax.axis_size("exp")
    holders = holder_count // EXPERTS
    outgoing = jnp.broadcast_to(
        buffer.reshape(EXPERTS, 1, CAP, width), (EXPERTS, holders, CAP, width)
    ).reshape(holder_count, CAP, width)
    gate_local = w_gate[0]
    up_local = w_up[0]
    down_local = w_down[0]
    arrived = lax.all_to_all(outgoing, "exp", split_axis=0, concat_axis=0, tiled=True)
    row_piece = lax.all_gather(arrived.reshape(-1, width), "req", axis=0, tiled=True)
    gate_proj = jnp.dot(row_piece, gate_local, preferred_element_type=jnp.float32)
    up_proj = jnp.dot(row_piece, up_local, preferred_element_type=jnp.float32)
    hidden = (jax.nn.silu(gate_proj) * up_proj).astype(jnp.bfloat16)
    summed_rows = lax.psum_scatter(
        jnp.dot(hidden, down_local, preferred_element_type=jnp.float32).astype(jnp.bfloat16),
        "req",
        scatter_dimension=0,
        tiled=True,
    )
    returned = lax.all_to_all(
        summed_rows.reshape(holder_count, CAP, width),
        "exp",
        split_axis=0,
        concat_axis=0,
        tiled=True,
    )
    expert_result = (
        returned.astype(jnp.float32)
        .reshape(EXPERTS, holders, CAP, width)
        .sum(axis=1)
        .reshape(EXPERTS * CAP, width)
    )
    picked = expert_result[target]
    layer_out = (
        (stream_rows + jnp.sum(gates[:, :, None] * picked, axis=1))
        .astype(jnp.bfloat16)
        .reshape(requests, tree_len, width)
    )
    kept_keys = jnp.take_along_axis(draft_keys, accepted_rows[:, :, None], axis=1)
    kept_values = jnp.take_along_axis(draft_values, accepted_rows[:, :, None], axis=1)
    accepted_cache = jnp.stack([kept_keys, kept_values], axis=1)
    return (attended, layer_out, accepted_cache)


def solution(mesh):
    return jax.shard_map(
        on_device,
        mesh=mesh,
        in_specs=(
            P(("req", "exp"), None, None),
            P(("req", "exp"), None, None),
            P(("req", "exp"), None, None),
            P(("req", "exp"), None),
            P(("req", "exp"), None, None),
            P(("req", "exp"), None, None),
            P(("req", "exp")),
            P("req", "exp", None),
            P("req", "exp", None),
            P(("req", "exp")),
            P(("req", "exp"), None, None),
            P(),
            P(),
            P("exp", None, "req"),
            P("exp", None, "req"),
            P("exp", "req", None),
            P(("req", "exp"), None, None),
            P(("req", "exp"), None),
        ),
        out_specs=(
            P(("req", "exp"), None, None),
            P(("req", "exp"), None, None),
            P(("req", "exp"), None, None, None),
        ),
        check_vma=False,
    )
```

time: 298 us -> 301 us (1.010)
  local copies, waits for them, and re-layouts: 71.3 us -> 14.1 us
  Pallas kernels: 0 us -> 49.5 us
  waiting for transfers between devices: 129 us -> 154 us
  matrix products: 50.2 us -> 27.9 us
  blocking collectives: 16.2 us -> 26.4 us
  other arithmetic: 11.3 us -> 6.65 us
  starting transfers between devices: 3.93 us -> 7.69 us
    pallas_call x0 -> x3, Pallas kernels: none -> 49.5 us  [the longest x1 24.2 us: attention(): pl.pallas_call(prompt_kernel, grid=(packs,), in_specs=[pl.BlockSpec((sour...]
    unnamed x48 -> x28, local copies, waits for them, and re-layouts: 27.5 us -> 1.97 us
    all_gather x2 -> x0, local copies, waits for them, and re-layouts: 24.9 us -> none  [the longest x1 12.5 us: on_device(): key_piece = lax.all_gather(prompt_keys, 'exp', axis=1, tiled=True)]
    dot_general x6 -> x0, matrix products: 22.8 us -> none  [the longest x1 7.34 us: on_device(): jnp.einsum('rhgk,gkhd->rhd', block_weights.astype(jnp.bfloat16), value_he...]
    all_gather x2 -> x1, waiting for transfers between devices: 14.3 us -> 32.4 us  [attention(): plane = lax.all_gather(sent, 'exp', axis=0, tiled=False)]
    all_to_all x0 -> x1, blocking collectives: none -> 10.4 us  [attention(): lax.all_to_all(pstat, 'exp', split_axis=0, concat_axis=0, tiled=True)]
    all_to_all x0 -> x1, waiting for transfers between devices: none -> 6.85 us  [attention(): part = lax.all_to_all(part, 'exp', split_axis=0, concat_axis=0, tiled=True)]
    reduce_sum x4 -> x0, other arithmetic: 6.82 us -> none  [the longest x1 3.97 us: on_device(): jnp.sum(cache_weights, axis=-1) + jnp.sum(tree_weights, axis=-1)]
  transfers between devices with their start and end apart: 5 -> 5, of which waited for: 4 -> 5; matrix products, arithmetic and copies ran while one was open for 24% -> 3% of each run, Pallas kernels for 0% -> 6%
where the time goes in v1:
time: 301 us; the launch traced here: 300 us
  waiting for transfers between devices  154 us (51%)
  Pallas kernels  49.5 us (16%)
  matrix products  27.9 us (9%)
  blocking collectives  26.4 us (9%)
  local copies, waits for them, and re-layouts  14.1 us (5%)
  between operations  14.1 us (5%)
  starting transfers between devices  7.69 us (3%)
  other arithmetic  6.65 us (2%)
    all_gather x1, waiting for transfers between devices, on_device(): lax.all_gather(arrived.reshape(-1, width), 'req', axis=0, tiled=True)  54.4 us
    reduce_scatter x1, waiting for transfers between devices, on_device(): lax.psum_scatter(jnp.dot(hidden, down_local, preferred_element_type=jnp.f...  48.1 us
    all_gather x1, waiting for transfers between devices, attention(): plane = lax.all_gather(sent, 'exp', axis=0, tiled=False)  32.4 us
    pallas_call x1, Pallas kernels, attention(): pl.pallas_call(prompt_kernel, grid=(packs,), in_specs=[pl.BlockSpec((sour...  24.2 us
    pallas_call x1, Pallas kernels, attention(): pl.pallas_call(local_kernel, grid_spec=pltpu.PrefetchScalarGridSpec(num_s...  19.5 us
    dot_general x1, matrix products, on_device(): jnp.dot(hidden, down_local, preferred_element_type=jnp.float32)  16.7 us
    all_to_all x1, blocking collectives, on_device(): lax.all_to_all(outgoing, 'exp', split_axis=0, concat_axis=0, tiled=True)  16 us
    all_to_all x1, waiting for transfers between devices, on_device(): lax.all_to_all(summed_rows.reshape(holder_count, CAP, width), 'exp', spli...  11.9 us
  transfers between devices with their start and end apart: 5, of which 5 were waited for; matrix products, arithmetic and copies ran while one was open for 3% of the time, Pallas kernels for 6%

profile of v1, /device:TPU:0, one launch (start us, length us, event | category | flops | bytes accessed | tf_op | source)
XLA Modules:
  0.0 300.1 jit_solution(7876533056497705185)
XLA Ops:
  8.1 1.7 pad_maximum_fusion
  9.9 32.4 %all-gather.6.cloned.1.call-done = bf16[512,2432]{1,0:T(8,128)(2,1)} async-done(((bf16[64,2432]{1,0:T(8,128)(2,1)}), bf16[512,2432]{1,0:T(8,128)(2,1)}) %all-gather.6.cloned.1.call-update) | async-done | bytes 2490384 | tf_op jit(solution)/shard_map/all_gather | solution.py:172
  42.3 24.2 %prompt_attention.1 = (bf16[8,64,2304]{2,1,0:T(8,128)(2,1)}, f32[8,64,128]{2,1,0:T(8,128)}) custom-call(bf16[8,64,2432]{2,1,0:T(8,128)(2,1)} %bitcast.74, bf16[8,64,2432]{2,1,0:T(8,128)(2,1)} %bitcast.75, bf16[2,64,2304]{2,1,0:T(8,128)(2,1)} %k_ref.1, bf16[2,64,2304]{2,1,0:T(8,128)(2,1)} %v_ref.1), custom_call_target="tpu_custom_call" | custom-call | tf_op jit(solution)/shard_map/prompt_attention/pallas_call | solution.py:199
  66.6 10.4 %all_to_all.20.pstat_ref = f32[8,64,128]{2,1,0:T(8,128)S(1)} all-to-all(f32[8,64,128]{2,1,0:T(8,128)} %get-tuple-element.12), channel_id=1, replica_groups=mesh['req'=4,'exp'=8] {'exp'}, dimensions={0} | all-to-all | bytes 524288 | tf_op jit(solution)/shard_map/all_to_all | solution.py:219
  76.9 3.6 %all-to-all-start = ((bf16[8,64,2304]{2,1,0:T(8,128)(2,1)}), bf16[8,64,2304]{2,1,0:T(8,128)(2,1)S(1)}, u32[]{:S(2)}, u32[]{:S(2)}) async-start(bf16[8,64,2304]{2,1,0:T(8,128)(2,1)} %get-tuple-element.11), calls=%async_computation | async-start | bytes 4718592 | tf_op jit(solution)/shard_map/all_to_all | solution.py:218
  83.1 19.5 %local_attention.1 = (f32[2,32,2304]{2,1,0:T(8,128)}, f32[2,32,128]{2,1,0:T(8,128)}) custom-call(s32[2]{0:T(128)} %len_ref.1, bf16[2,32,2304]{2,1,0:T(8,128)(2,1)} %q_ref.1, bf16[2,768,2304]{2,1,0:T(8,128)(2,1)} %kc_ref.1, bf16[2,768,2304]{2,1,0:T(8,128)(2,1)} %vc_ref.1, bf16[2,32,2304]{2,1,0:T(8,128)(2,1)} %kd_ref.1, bf16[2,32,2304]{2,1,0:T(8,128)(2,1)} %vd_ref.1, ...), custom_call_target="tpu_custom_call" | custom-call | flops 1887436800 | bytes 14155776 | tf_op jit(solution)/shard_map/local_attention/pallas_call | solution.py:177
  103.1 6.8 %all-to-all-done.part_ref = bf16[8,64,2304]{2,1,0:T(8,128)(2,1)S(1)} async-done(((bf16[8,64,2304]{2,1,0:T(8,128)(2,1)}), bf16[8,64,2304]{2,1,0:T(8,128)(2,1)S(1)}, u32[]{:S(2)}, u32[]{:S(2)}) %all-to-all-start) | async-done | bytes 2359328 | tf_op jit(solution)/shard_map/all_to_all | solution.py:218
  110.0 1.1 copy-done.1
  111.8 5.7 %merge.1 = (bf16[64,2304]{1,0:T(8,128)(2,1)}, bf16[64,2304]{1,0:T(8,128)(2,1)S(1)}, bf16[64,2304]{1,0:T(8,128)(2,1)S(1)}) custom-call(bf16[8,64,2304]{2,1,0:T(8,128)(2,1)S(1)} %all-to-all-done.part_ref, f32[8,64,128]{2,1,0:T(8,128)S(1)} %all_to_all.20.pstat_ref, f32[64,2304]{1,0:T(8,128)S(1)} %bitcast.71, f32[64,128]{1,0:T(8,128)S(1)} %bitcast.73, ...), custom_call_target="tpu_custom_call" | custom-call | tf_op jit(solution)/shard_map/merge/pallas_call | solution.py:220
  118.1 1.7 scatter_custom_fusion
  120.0 16.0 %all_to_all.21 = bf16[8,18,2304]{2,1,0:T(8,128)(2,1)S(1)} all-to-all(bf16[8,18,2304]{2,1,0:T(8,128)(2,1)S(1)} %reshape_reshape.3), channel_id=1, replica_groups=mesh['req'=4,'exp'=8] {'exp'}, dimensions={0} | all-to-all | bytes 1327104 | tf_op jit(solution)/shard_map/all_to_all | solution.py:278
  136.0 1.0 reshape.178
  137.3 54.4 %all-gather.4.cloned.1.call-done = bf16[576,2304]{1,0:T(8,128)(2,1)} async-done(((bf16[144,2304]{1,0:T(8,128)(2,1)}), bf16[576,2304]{1,0:T(8,128)(2,1)}) %all-gather.4.cloned.1.call-update) | async-done | bytes 2654224 | tf_op jit(solution)/shard_map/all_gather | solution.py:279
  191.7 9.7 %fusion.4 = f32[576,1440]{1,0:T(8,128)} fusion(bf16[576,2304]{1,0:T(8,128)(2,1)} %all-gather.4.cloned.1.call-done, bf16[1,2304,1440]{1,2,0:T(8,128)(2,1)} %param.33), kind=kOutput, calls=%fused_computation.9 | convolution fusion | flops 3822059520 | bytes 12607488 | tf_op jit(solution)/shard_map/dot_general | solution.py:280
  201.4 16.7 %fusion.6 = bf16[576,2304]{1,0:T(8,128)(2,1)} fusion(bf16[1,1440,2304]{2,1,0:T(8,128)(2,1)} %param.35, f32[576,1440]{1,0:T(8,128)} %fusion.4, bf16[576,2304]{1,0:T(8,128)(2,1)} %all-gather.4.cloned.1.call-done, bf16[1,2304,1440]{1,2,0:T(8,128)(2,1)} %param.34), kind=kOutput, calls=%fused_computation.11 | convolution fusion | flops 7650422784 | bytes 21897216 | tf_op jit(solution)/shard_map/dot_general | solution.py:284
  218.5 0.8 gather_fusion.2
  219.3 0.8 gather_fusion.3
  221.5 48.1 %reduce-scatter.2.cloned.1.call-done = bf16[144,2304]{1,0:T(8,128)(2,1)} async-done(((bf16[576,2304]{1,0:T(8,128)(2,1)}), bf16[144,2304]{1,0:T(8,128)(2,1)}) %reduce-scatter.2.cloned.1.call-update) | async-done | bytes 663568 | tf_op jit(solution)/shard_map/reduce_scatter | solution.py:283
  269.7 2.2 reshape.179
  271.9 3.8 %all-to-all-start.3 = ((bf16[8,18,2304]{2,1,0:T(8,128)(2,1)}), bf16[8,18,2304]{2,1,0:T(8,128)(2,1)S(1)}, u32[]{:S(2)}, u32[]{:S(2)}) async-start(bf16[8,18,2304]{2,1,0:T(8,128)(2,1)} %reshape.179), calls=%async_computation.4 | async-start | bytes 1769472 | tf_op jit(solution)/shard_map/all_to_all | solution.py:289
  275.8 1.1 gather_fusion.1
  277.2 11.9 %all-to-all-done.3 = bf16[8,18,2304]{2,1,0:T(8,128)(2,1)S(1)} async-done(((bf16[8,18,2304]{2,1,0:T(8,128)(2,1)}), bf16[8,18,2304]{2,1,0:T(8,128)(2,1)S(1)}, u32[]{:S(2)}, u32[]{:S(2)}) %all-to-all-start.3) | async-done | bytes 663584 | tf_op jit(solution)/shard_map/all_to_all | solution.py:289
  289.3 1.1 gather_fusion
  291.1 1.7 multiply_reduce_fusion
  (84 shorter events, 9.5 us)
Async XLA Ops:
  7.2 268.5 %copy-start = (bf16[2304,8]{0,1:T(8,128)(2,1)S(1)}, bf16[2304,8]{0,1:T(8,128)(2,1)}, u32[]{:S(2)}) copy-start(bf16[2304,8]{0,1:T(8,128)(2,1)} %param.32) | copy-start | bytes 110596
  7.2 35.1 %all-gather.6.cloned.1.call-start = ((), (), s32[]{:S(2)}) async-start(), calls=%async_computation.7 | async-start | bytes 2801664 | tf_op jit(solution)/shard_map/all_gather | solution.py:172
  66.5 14.1 %copy-start.6 = (s32[2,32,2]{1,2,0:T(2,128)S(1)}, s32[2,32,2]{1,2,0:T(2,128)}, u32[]{:S(2)}) copy-start(s32[2,32,2]{1,2,0:T(2,128)} %param.36) | copy-start | bytes 1540
  66.5 14.2 %copy-start.8 = (f32[2304]{0:T(1024)S(1)}, f32[2304]{0:T(1024)}, u32[]{:S(2)}) copy-start(f32[2304]{0:T(1024)} %param.31) | copy-start | bytes 27652
  66.5 14.9 %copy-start.12 = (s32[2,32]{1,0:T(2,128)S(1)}, s32[2,32]{1,0:T(2,128)}, u32[]{:S(2)}) copy-start(s32[2,32]{1,0:T(2,128)} %param.23) | copy-start | bytes 772
  76.9 33.0 %all-to-all-start = ((bf16[8,64,2304]{2,1,0:T(8,128)(2,1)}), bf16[8,64,2304]{2,1,0:T(8,128)(2,1)S(1)}, u32[]{:S(2)}, u32[]{:S(2)}) async-start(bf16[8,64,2304]{2,1,0:T(8,128)(2,1)} %get-tuple-element.11), calls=%async_computation | async-start | bytes 4718592 | tf_op jit(solution)/shard_map/all_to_all | solution.py:218
  80.6 111.1 %all-gather.4.cloned.1.call-start = ((), (), s32[]{:S(2)}) async-start(), calls=%async_computation.5 | async-start | bytes 3317760 | tf_op jit(solution)/shard_map/all_gather | solution.py:279
  83.1 19.5 %copy-start.9 = (s32[128]{0:T(128)}, s32[128]{0:T(128)S(1)}, u32[]{:S(2)}) copy-start(s32[128]{0:T(128)S(1)} %select_reduce_fusion) | copy-start | bytes 1540
  83.1 26.9 %copy-start.2 = (bf16[2,32,2304]{2,1,0:T(8,128)(2,1)S(1)}, bf16[2,32,2304]{2,1,0:T(8,128)(2,1)}, u32[]{:S(2)}) copy-start(bf16[2,32,2304]{2,1,0:T(8,128)(2,1)} %param.30) | copy-start | bytes 884740
  110.0 1.1 copy-start.1
  111.0 0.8 copy-start.3
  137.1 132.6 %reduce-scatter.2.cloned.1.call-start = ((), (), s32[]{:S(2)}) async-start(), calls=%async_computation.6 | async-start | bytes 3317760 | tf_op jit(solution)/shard_map/reduce_scatter | solution.py:283
  201.4 16.7 %copy-start.10 = (s32[128]{0:T(128)S(1)}, s32[128]{0:T(128)}, u32[]{:S(2)}) copy-start(s32[128]{0:T(128)} %copy-done.9) | copy-start | bytes 1540
  201.4 16.8 %copy-start.7 = (s32[2,32,2]{1,2,0:T(2,128)S(1)}, s32[2,32,2]{1,2,0:T(2,128)}, u32[]{:S(2)}) copy-start(s32[2,32,2]{1,2,0:T(2,128)} %param.36) | copy-start | bytes 1540
  201.4 17.0 %copy-start.11 = (s32[2,8]{1,0:T(2,128)S(1)}, s32[2,8]{1,0:T(2,128)}, u32[]{:S(2)}) copy-start(s32[2,8]{1,0:T(2,128)} %param.37) | copy-start | bytes 196
  201.4 17.1 %copy-start.4 = (bf16[2,32,2304]{2,1,0:T(8,128)(2,1)S(1)}, bf16[2,32,2304]{2,1,0:T(8,128)(2,1)}, u32[]{:S(2)}) copy-start(bf16[2,32,2304]{2,1,0:T(8,128)(2,1)} %kd_ref.1) | copy-start | bytes 884740
  218.1 1.3 copy-start.5
  271.9 17.3 %all-to-all-start.3 = ((bf16[8,18,2304]{2,1,0:T(8,128)(2,1)}), bf16[8,18,2304]{2,1,0:T(8,128)(2,1)S(1)}, u32[]{:S(2)}, u32[]{:S(2)}) async-start(bf16[8,18,2304]{2,1,0:T(8,128)(2,1)} %reshape.179), calls=%async_computation.4 | async-start | bytes 1769472 | tf_op jit(solution)/shard_map/all_to_all | solution.py:289
Sparse Core Ops, SparseCore 0:
  10.0 32.2 all-gather.5
  137.2 54.4 all-gather.3
  218.2 51.3 reduce-scatter.1

commit v2 on v1

--- a/solution.py
+++ b/solution.py
@@ -1,3 +1,5 @@
+import functools
+
 import jax
 import jax.numpy as jnp
 from jax import lax
@@ -228,6 +230,182 @@
     )
 
 
+def greet(peers):
+    barrier = pltpu.get_barrier_semaphore()
+    for axis, size in peers:
+        me = lax.axis_index(axis)
+        for step in range(1, size):
+            pl.semaphore_signal(
+                barrier, inc=1, device_id={axis: lax.rem(me + step, size)},
+                device_id_type=pl.DeviceIdType.MESH,
+            )
+    pl.semaphore_wait(barrier, sum(size - 1 for _, size in peers))
+
+
+def remote(src, dst, send, recv, axis, target):
+    return pltpu.make_async_remote_copy(
+        src_ref=src, dst_ref=dst, send_sem=send, recv_sem=recv, device_id={axis: target},
+        device_id_type=pl.DeviceIdType.MESH,
+    )
+
+
+def dispatch_kernel(
+    depth, size, rows_ref, pick_ref, out_ref, held, staged, zsend, zrecv, psend, precv, own
+):
+    z, e = lax.axis_index("req"), lax.axis_index("exp")
+    experts, cap = pick_ref.shape[1], pick_ref.shape[2]
+    holders = size // experts
+    greet((("req", depth), ("exp", size)))
+    along = []
+    for k in range(1, depth):
+        copy = remote(
+            rows_ref, held.at[k - 1], zsend.at[k - 1], zrecv.at[k - 1], "req",
+            lax.rem(z + k, depth),
+        )
+        copy.start()
+        along.append(copy)
+    started, locals_ = [], []
+    for k in range(depth):
+        source = lax.rem(z - k + depth, depth)
+        if k:
+            along[k - 1].wait_recv()
+        rows = rows_ref[...] if k == 0 else held[k - 1]
+        for x in range(experts):
+            staged[k, x] = jnp.dot(
+                pick_ref[source, x], rows, preferred_element_type=jnp.float32
+            ).astype(jnp.bfloat16)
+        for o in range(1, size):
+            target = lax.rem(e + o, size)
+            copy = remote(
+                staged.at[k, target // holders], out_ref.at[source, e], psend.at[k, o - 1],
+                precv.at[k, o - 1], "exp", target,
+            )
+            copy.start()
+            started.append((copy, k, o, source))
+        copy = pltpu.make_async_copy(staged.at[k, e // holders], out_ref.at[source, e], own.at[k])
+        copy.start()
+        locals_.append(copy)
+    for copy in along:
+        copy.wait_send()
+    for copy in locals_:
+        copy.wait()
+    for copy, k, o, source in started:
+        copy.wait_send()
+        origin = lax.rem(e - o + size, size)
+        remote(
+            staged.at[k, 0], out_ref.at[source, origin], psend.at[k, o - 1], precv.at[k, o - 1],
+            "exp", origin,
+        ).wait_recv()
+
+
+def collect_kernel(
+    depth, size, y_ref, mix_ref, stream_ref, out_ref, landed, partial, held,
+    zsend, zrecv, psend, precv, own,
+):
+    z, e = lax.axis_index("req"), lax.axis_index("exp")
+    experts = mix_ref.shape[1]
+    rows = stream_ref.shape[0]
+    holders = size // experts
+    greet((("req", depth), ("exp", size)))
+    started = []
+    order = list(range(1, depth)) + [0]
+    for k in order:
+        home = lax.rem(z + k, depth)
+        group = []
+        for o in range(1, size):
+            target = lax.rem(e + o, size)
+            copy = remote(
+                y_ref.at[home, target], landed.at[k, e], psend.at[k, o - 1], precv.at[k, o - 1],
+                "exp", target,
+            )
+            copy.start()
+            group.append(copy)
+        copy = pltpu.make_async_copy(y_ref.at[home, e], landed.at[k, e], own.at[k])
+        copy.start()
+        started.append((k, home, group, copy))
+    along = []
+    for k, home, group, mine in started:
+        mine.wait()
+        for o in range(1, size):
+            origin = lax.rem(e - o + size, size)
+            remote(
+                y_ref.at[home, origin], landed.at[k, origin], psend.at[k, o - 1],
+                precv.at[k, o - 1], "exp", origin,
+            ).wait_recv()
+        total = None
+        for s in range(size):
+            both = jnp.dot(
+                mix_ref[home, s // holders], landed[k, s], preferred_element_type=jnp.float32
+            )
+            total = both if total is None else total + both
+        total = total[:rows] + total[rows:]
+        if k == 0:
+            kept = total + stream_ref[...].astype(jnp.float32)
+        else:
+            partial[k - 1] = total.astype(jnp.bfloat16)
+            copy = remote(
+                partial.at[k - 1], held.at[k - 1], zsend.at[k - 1], zrecv.at[k - 1], "req", home
+            )
+            copy.start()
+            along.append(copy)
+    for i, copy in enumerate(along):
+        copy.wait_recv()
+        kept += held[i].astype(jnp.float32)
+    out_ref[...] = kept.astype(jnp.bfloat16)
+    for copy in along:
+        copy.wait_send()
+    for _, _, group, _ in started:
+        for copy in group:
+            copy.wait_send()
+
+
+def dispatch(normed, pick, depth, size):
+    rows, width = normed.shape
+    cap = pick.shape[2]
+    dma = pltpu.SemaphoreType.DMA
+    vmem = pl.BlockSpec(memory_space=pltpu.VMEM)
+    return pl.pallas_call(
+        functools.partial(dispatch_kernel, depth, size),
+        out_shape=jax.ShapeDtypeStruct((depth, size, cap, width), jnp.bfloat16),
+        in_specs=[vmem, vmem],
+        out_specs=pl.BlockSpec(memory_space=pl.ANY),
+        scratch_shapes=[
+            pltpu.VMEM((depth - 1, rows, width), jnp.bfloat16),
+            pltpu.VMEM((depth, pick.shape[1], cap, width), jnp.bfloat16),
+            dma((depth - 1,)), dma((depth - 1,)),
+            dma((depth, size - 1)), dma((depth, size - 1)), dma((depth,)),
+        ],
+        compiler_params=pltpu.CompilerParams(
+            collective_id=0, has_side_effects=True, vmem_limit_bytes=40 * 1024 * 1024
+        ),
+        name="dispatch",
+    )(normed, pick)
+
+
+def collect(y, mix, stream, depth, size):
+    rows, width = stream.shape
+    cap = y.shape[2]
+    dma = pltpu.SemaphoreType.DMA
+    vmem = pl.BlockSpec(memory_space=pltpu.VMEM)
+    return pl.pallas_call(
+        functools.partial(collect_kernel, depth, size),
+        out_shape=jax.ShapeDtypeStruct((rows, width), jnp.bfloat16),
+        in_specs=[pl.BlockSpec(memory_space=pl.ANY), vmem, vmem],
+        out_specs=vmem,
+        scratch_shapes=[
+            pltpu.VMEM((depth, size, cap, width), jnp.bfloat16),
+            pltpu.VMEM((depth - 1, rows, width), jnp.bfloat16),
+            pltpu.VMEM((depth - 1, rows, width), jnp.bfloat16),
+            dma((depth - 1,)), dma((depth - 1,)),
+            dma((depth, size - 1)), dma((depth, size - 1)), dma((depth,)),
+        ],
+        compiler_params=pltpu.CompilerParams(
+            collective_id=1, has_side_effects=True, vmem_limit_bytes=48 * 1024 * 1024
+        ),
+        name="collect",
+    )(y, mix, stream)
+
+
 def on_device(
     queries,
     draft_keys,
@@ -255,56 +433,34 @@
         prompt_keys, prompt_values, group_ids, residual, norm_gain,
     )
     attended = attended.reshape(requests, tree_len, width)
-    stream_rows = stream.astype(jnp.float32)
     logits = jnp.dot(normed, router, preferred_element_type=jnp.float32)
     routed = expert_ids.reshape(row_count, TOPK)
     chosen = jnp.take_along_axis(logits, routed, axis=1)
     gate_first = 1.0 / (1.0 + jnp.exp(chosen[:, 1] - chosen[:, 0]))
     gates = jnp.stack([gate_first, 1.0 - gate_first], axis=1)
-    target = routed * CAP + slot_numbers(routed)
-    buffer = (
-        jnp.zeros((EXPERTS * CAP, width), jnp.bfloat16)
-        .at[target.reshape(-1)]
-        .set(jnp.repeat(normed, TOPK, axis=0))
-    )
-    holder_count = lax.axis_size("exp")
-    holders = holder_count // EXPERTS
-    outgoing = jnp.broadcast_to(
-        buffer.reshape(EXPERTS, 1, CAP, width), (EXPERTS, holders, CAP, width)
-    ).reshape(holder_count, CAP, width)
-    gate_local = w_gate[0]
-    up_local = w_up[0]
-    down_local = w_down[0]
-    arrived = lax.all_to_all(outgoing, "exp", split_axis=0, concat_axis=0, tiled=True)
-    row_piece = lax.all_gather(arrived.reshape(-1, width), "req", axis=0, tiled=True)
-    gate_proj = jnp.dot(row_piece, gate_local, preferred_element_type=jnp.float32)
-    up_proj = jnp.dot(row_piece, up_local, preferred_element_type=jnp.float32)
+    depth, size = lax.axis_size("req"), lax.axis_size("exp")
+    all_routed = lax.all_gather(routed, "req", axis=0, tiled=False)
+    all_gates = lax.all_gather(gates, "req", axis=0, tiled=False)
+    target = all_routed * CAP + jax.vmap(slot_numbers)(all_routed)
+    slots = jnp.arange(EXPERTS * CAP, dtype=jnp.int32).reshape(EXPERTS, CAP)
+    pick = (target[:, None, None, :, 0] == slots[None, :, :, None]) | (
+        target[:, None, None, :, 1] == slots[None, :, :, None]
+    )
+    pick = pick.astype(jnp.bfloat16)
+    hit = target[:, None, :, None, :] == slots[None, :, None, :, None]
+    mix = jnp.sum(jnp.where(hit, all_gates[:, None, :, None, :], 0.0), axis=-1)
+    mix_high = mix.astype(jnp.bfloat16)
+    mix_low = (mix - lax.reduce_precision(mix, 8, 7)).astype(jnp.bfloat16)
+    mix = jnp.concatenate([mix_high, mix_low], axis=2)
+    arrived = dispatch(normed, pick, depth, size)
+    row_piece = arrived.reshape(-1, width)
+    gate_proj = jnp.dot(row_piece, w_gate[0], preferred_element_type=jnp.float32)
+    up_proj = jnp.dot(row_piece, w_up[0], preferred_element_type=jnp.float32)
     hidden = (jax.nn.silu(gate_proj) * up_proj).astype(jnp.bfloat16)
-    summed_rows = lax.psum_scatter(
-        jnp.dot(hidden, down_local, preferred_element_type=jnp.float32).astype(jnp.bfloat16),
-        "req",
-        scatter_dimension=0,
-        tiled=True,
-    )
-    returned = lax.all_to_all(
-        summed_rows.reshape(holder_count, CAP, width),
-        "exp",
-        split_axis=0,
-        concat_axis=0,
-        tiled=True,
-    )
-    expert_result = (
-        returned.astype(jnp.float32)
-        .reshape(EXPERTS, holders, CAP, width)
-        .sum(axis=1)
-        .reshape(EXPERTS * CAP, width)
-    )
-    picked = expert_result[target]
-    layer_out = (
-        (stream_rows + jnp.sum(gates[:, :, None] * picked, axis=1))
-        .astype(jnp.bfloat16)
-        .reshape(requests, tree_len, width)
-    )
+    pieces = jnp.dot(hidden, w_down[0], preferred_element_type=jnp.float32).astype(jnp.bfloat16)
+    layer_out = collect(
+        pieces.reshape(depth, size, CAP, width), mix, stream, depth, size
+    ).reshape(requests, tree_len, width)
     kept_keys = jnp.take_along_axis(draft_keys, accepted_rows[:, :, None], axis=1)
     kept_values = jnp.take_along_axis(draft_values, accepted_rows[:, :, None], axis=1)
     accepted_cache = jnp.stack([kept_keys, kept_values], axis=1)

time: 301 us -> 273 us (0.907)
  waiting for transfers between devices: 154 us -> 28.7 us
  Pallas kernels: 49.5 us -> 139 us
  local copies, waits for them, and re-layouts: 14.1 us -> 21.6 us
    pallas_call x0 -> x2, Pallas kernels: none -> 89.1 us  [the longest x1 45.3 us: collect(): pl.pallas_call(functools.partial(collect_kernel, depth, size), out_shape=...]
    all_gather x1 -> x0, waiting for transfers between devices: 54.4 us -> none  [on_device(): lax.all_gather(arrived.reshape(-1, width), 'req', axis=0, tiled=True)]
    reduce_scatter x1 -> x0, waiting for transfers between devices: 48.1 us -> none  [on_device(): lax.psum_scatter(jnp.dot(hidden, down_local, preferred_element_type=jnp.f...]
    all_gather x0 -> x2, blocking collectives: none -> 28 us  [the longest x1 15.4 us: on_device(): all_gates = lax.all_gather(gates, 'req', axis=0, tiled=False)]
    all_to_all x2 -> x0, blocking collectives: 26.4 us -> none  [the longest x1 16 us: on_device(): lax.all_to_all(outgoing, 'exp', split_axis=0, concat_axis=0, tiled=True)]
    all_gather x1, waiting for transfers between devices: 32.4 us -> 16.1 us  [attention(): plane = lax.all_gather(sent, 'exp', axis=0, tiled=False)]
    unnamed x28 -> x22, local copies, waits for them, and re-layouts: 1.97 us -> 7.95 us
    all_to_all x1, waiting for transfers between devices: 11.9 us -> 6.06 us  [attention(): lax.all_to_all(pstat, 'exp', split_axis=0, concat_axis=0, tiled=True)]
  transfers between devices with their start and end apart: 5 -> 3, of which waited for: 5 -> 3; matrix products, arithmetic and copies ran while one was open for 3% -> 3% of each run, Pallas kernels for 6% -> 7%
where the time goes in v2:
time: 273 us; the launch traced here: 272 us
  Pallas kernels  139 us (51%)
  waiting for transfers between devices  28.7 us (11%)
  matrix products  28.7 us (11%)
  blocking collectives  28 us (10%)
  local copies, waits for them, and re-layouts  21.6 us (8%)
  between operations  14.3 us (5%)
  starting transfers between devices  7.21 us (3%)
  other arithmetic  5.05 us (2%)
    pallas_call x1, Pallas kernels, collect(): pl.pallas_call(functools.partial(collect_kernel, depth, size), out_shape=...  45.3 us
    pallas_call x1, Pallas kernels, dispatch(): pl.pallas_call(functools.partial(dispatch_kernel, depth, size), out_shape...  43.8 us
    pallas_call x1, Pallas kernels, attention(): pl.pallas_call(prompt_kernel, grid=(packs,), in_specs=[pl.BlockSpec((sour...  24.3 us
    pallas_call x1, Pallas kernels, attention(): pl.pallas_call(local_kernel, grid_spec=pltpu.PrefetchScalarGridSpec(num_s...  19.5 us
    dot_general x1, matrix products, on_device(): jnp.dot(hidden, w_down[0], preferred_element_type=jnp.float32)  16.7 us
    all_gather x1, waiting for transfers between devices, attention(): plane = lax.all_gather(sent, 'exp', axis=0, tiled=False)  16.1 us
    all_gather x1, blocking collectives, on_device(): all_gates = lax.all_gather(gates, 'req', axis=0, tiled=False)  15.4 us
    all_gather x1, blocking collectives, on_device(): all_routed = lax.all_gather(routed, 'req', axis=0, tiled=False)  12.6 us
  transfers between devices with their start and end apart: 3, of which 3 were waited for; matrix products, arithmetic and copies ran while one was open for 3% of the time, Pallas kernels for 7%

profile of v2, /device:TPU:0, one launch (start us, length us, event | category | flops | bytes accessed | tf_op | source)
XLA Modules:
  0.0 272.0 jit_solution(6081029176656547715)
XLA Ops:
  8.1 1.7 pad_maximum_fusion
  10.7 12.6 %all_gather.17 = s32[4,64,2]{1,2,0:T(2,128)S(1)} all-gather(s32[1,64,2]{1,2,0:T(2,128)S(1)} %all_gather_reshape.3), channel_id=1, replica_groups=mesh['req'=4,'exp'=8] {'req'}, dimensions={0}, use_global_device_ids=true | all-gather | bytes 2560 | tf_op jit(solution)/shard_map/all_gather | solution.py:442
  23.9 1.0 fusion.26
  26.1 16.1 %all-gather.5.cloned.1.call-done = bf16[512,2432]{1,0:T(8,128)(2,1)} async-done(((bf16[64,2432]{1,0:T(8,128)(2,1)}), bf16[512,2432]{1,0:T(8,128)(2,1)}) %all-gather.5.cloned.1.call-update) | async-done | bytes 2490384 | tf_op jit(solution)/shard_map/all_gather | solution.py:174
  42.3 24.3 %prompt_attention.1 = (bf16[8,64,2304]{2,1,0:T(8,128)(2,1)}, f32[8,64,128]{2,1,0:T(8,128)}) custom-call(bf16[8,64,2432]{2,1,0:T(8,128)(2,1)} %bitcast.77, bf16[8,64,2432]{2,1,0:T(8,128)(2,1)} %bitcast.78, bf16[2,64,2304]{2,1,0:T(8,128)(2,1)} %k_ref.1, bf16[2,64,2304]{2,1,0:T(8,128)(2,1)} %v_ref.1), custom_call_target="tpu_custom_call" | custom-call | tf_op jit(solution)/shard_map/prompt_attention/pallas_call | solution.py:201
  66.5 3.6 %all-to-all-start.1 = ((f32[8,64,128]{2,1,0:T(8,128)}), f32[8,64,128]{2,1,0:T(8,128)S(1)}, u32[]{:S(2)}, u32[]{:S(2)}) async-start(f32[8,64,128]{2,1,0:T(8,128)} %get-tuple-element.12), calls=%async_computation.1 | async-start | bytes 524288 | tf_op jit(solution)/shard_map/all_to_all | solution.py:221
  70.9 6.1 %all-to-all-done.1.pstat_ref = f32[8,64,128]{2,1,0:T(8,128)S(1)} async-done(((f32[8,64,128]{2,1,0:T(8,128)}), f32[8,64,128]{2,1,0:T(8,128)S(1)}, u32[]{:S(2)}, u32[]{:S(2)}) %all-to-all-start.1) | async-done | bytes 262176 | tf_op jit(solution)/shard_map/all_to_all | solution.py:221
  77.0 3.6 %all-to-all-start = ((bf16[8,64,2304]{2,1,0:T(8,128)(2,1)}), bf16[8,64,2304]{2,1,0:T(8,128)(2,1)S(1)}, u32[]{:S(2)}, u32[]{:S(2)}) async-start(bf16[8,64,2304]{2,1,0:T(8,128)(2,1)} %get-tuple-element.11), calls=%async_computation | async-start | bytes 4718592 | tf_op jit(solution)/shard_map/all_to_all | solution.py:220
  81.6 0.8 gather_fusion.2
  83.1 19.5 %local_attention.1 = (f32[2,32,2304]{2,1,0:T(8,128)}, f32[2,32,128]{2,1,0:T(8,128)}) custom-call(s32[2]{0:T(128)} %len_ref.1, bf16[2,32,2304]{2,1,0:T(8,128)(2,1)} %q_ref.1, bf16[2,768,2304]{2,1,0:T(8,128)(2,1)} %kc_ref.1, bf16[2,768,2304]{2,1,0:T(8,128)(2,1)} %vc_ref.1, bf16[2,32,2304]{2,1,0:T(8,128)(2,1)} %kd_ref.1, bf16[2,32,2304]{2,1,0:T(8,128)(2,1)} %vd_ref.1, ...), custom_call_target="tpu_custom_call" | custom-call | flops 1887436800 | bytes 14155776 | tf_op jit(solution)/shard_map/local_attention/pallas_call | solution.py:179
  103.6 6.4 %all-to-all-done.part_ref = bf16[8,64,2304]{2,1,0:T(8,128)(2,1)S(1)} async-done(((bf16[8,64,2304]{2,1,0:T(8,128)(2,1)}), bf16[8,64,2304]{2,1,0:T(8,128)(2,1)S(1)}, u32[]{:S(2)}, u32[]{:S(2)}) %all-to-all-start) | async-done | bytes 2359328 | tf_op jit(solution)/shard_map/all_to_all | solution.py:220
  110.0 1.1 copy-done.3
  111.0 1.0 copy-done.4
  112.8 5.7 %merge.1 = (bf16[64,2304]{1,0:T(8,128)(2,1)}, bf16[64,2304]{1,0:T(8,128)(2,1)S(1)}, bf16[64,2304]{1,0:T(8,128)(2,1)S(1)}) custom-call(bf16[8,64,2304]{2,1,0:T(8,128)(2,1)S(1)} %all-to-all-done.part_ref, f32[8,64,128]{2,1,0:T(8,128)S(1)} %all-to-all-done.1.pstat_ref, f32[64,2304]{1,0:T(8,128)S(1)} %bitcast.74, f32[64,128]{1,0:T(8,128)S(1)} %bitcast.76, ...), custom_call_target="tpu_custom_call" | custom-call | tf_op jit(solution)/shard_map/merge/pallas_call | solution.py:222
  118.5 43.8 %dispatch.1 = bf16[4,8,18,2304]{3,2,1,0:T(8,128)(2,1)S(1)} custom-call(bf16[64,2304]{1,0:T(8,128)(2,1)S(1)} %get-tuple-element.16.rows_ref, bf16[4,8,18,64]{3,2,1,0:T(8,128)(2,1)S(1)} %or_convert_fusion.pick_ref), custom_call_target="tpu_custom_call" | custom-call | tf_op jit(solution)/shard_map/dispatch/pallas_call | solution.py:367
  162.4 1.7 copy-done.2
  164.1 4.5 %reshape.131 = bf16[576,2304]{1,0:T(8,128)(2,1)} reshape(bf16[4,8,18,2304]{3,2,1,0:T(8,128)(2,1)} %copy-done.2) | data formatting | bytes 5308416 | tf_op jit(solution)/shard_map/reshape | solution.py:456
  168.6 9.7 %fusion.4 = f32[576,1440]{1,0:T(8,128)} fusion(bf16[576,2304]{1,0:T(8,128)(2,1)} %reshape.131, bf16[1,2304,1440]{1,2,0:T(8,128)(2,1)} %param.33), kind=kOutput, calls=%fused_computation.7 | convolution fusion | flops 3822059520 | bytes 12607488 | tf_op jit(solution)/shard_map/dot_general | solution.py:457
  178.4 16.7 %fusion.6 = bf16[576,2304]{1,0:T(8,128)(2,1)} fusion(bf16[1,1440,2304]{2,1,0:T(8,128)(2,1)} %param.35, f32[576,1440]{1,0:T(8,128)} %fusion.4, bf16[576,2304]{1,0:T(8,128)(2,1)} %reshape.131, bf16[1,2304,1440]{1,2,0:T(8,128)(2,1)} %param.34), kind=kOutput, calls=%fused_computation.9 | convolution fusion | flops 7650422784 | bytes 21897216 | tf_op jit(solution)/shard_map/dot_general | solution.py:460
  195.0 4.5 %reshape.132.y_ref = bf16[4,8,18,2304]{3,2,1,0:T(8,128)(2,1)} reshape(bf16[576,2304]{1,0:T(8,128)(2,1)} %fusion.6) | data formatting | bytes 5308416 | tf_op jit(solution)/shard_map/reshape | solution.py:462
  199.7 1.1 gather_fusion
  201.0 15.4 %all-gather.2 = f32[4,64,2]{1,2,0:T(2,128)S(1)} all-gather(f32[1,64,2]{1,2,0:T(2,128)S(1)} %maximum_bitcast_fusion), channel_id=3, replica_groups=mesh['req'=4,'exp'=8] {'req'}, dimensions={0}, use_global_device_ids=true | all-gather | bytes 2560 | tf_op jit(solution)/shard_map/all_gather | solution.py:443
  217.2 2.0 copy-done.1
  219.2 45.3 %collect.1 = bf16[64,2304]{1,0:T(8,128)(2,1)S(1)} custom-call(bf16[4,8,18,2304]{3,2,1,0:T(8,128)(2,1)S(1)} %copy-done.1, bf16[4,8,128,18]{3,2,1,0:T(8,128)(2,1)S(1)} %copy.80.mix_ref, bf16[64,2304]{1,0:T(8,128)(2,1)S(1)} %get-tuple-element.17.stream_ref), custom_call_target="tpu_custom_call" | custom-call | tf_op jit(solution)/shard_map/collect/pallas_call | solution.py:390
  (69 shorter events, 9.7 us)
Async XLA Ops:
  7.2 192.3 %copy-start = (bf16[2304,8]{0,1:T(8,128)(2,1)S(1)}, bf16[2304,8]{0,1:T(8,128)(2,1)}, u32[]{:S(2)}) copy-start(bf16[2304,8]{0,1:T(8,128)(2,1)} %param.32) | copy-start | bytes 110596
  7.2 35.1 %all-gather.5.cloned.1.call-start = ((), (), s32[]{:S(2)}) async-start(), calls=%async_computation.2 | async-start | bytes 2801664 | tf_op jit(solution)/shard_map/all_gather | solution.py:174
  25.0 45.5 %copy-start.8 = (f32[2304]{0:T(1024)S(1)}, f32[2304]{0:T(1024)}, u32[]{:S(2)}) copy-start(f32[2304]{0:T(1024)} %param.31) | copy-start | bytes 27652
  66.5 14.2 %copy-start.6 = (bf16[2,32,2304]{2,1,0:T(8,128)(2,1)S(1)}, bf16[2,32,2304]{2,1,0:T(8,128)(2,1)}, u32[]{:S(2)}) copy-start(bf16[2,32,2304]{2,1,0:T(8,128)(2,1)} %kd_ref.1) | copy-start | bytes 884740
  66.5 15.1 %copy-start.7 = (bf16[2,32,2304]{2,1,0:T(8,128)(2,1)S(1)}, bf16[2,32,2304]{2,1,0:T(8,128)(2,1)}, u32[]{:S(2)}) copy-start(bf16[2,32,2304]{2,1,0:T(8,128)(2,1)} %vd_ref.1) | copy-start | bytes 884740
  66.5 10.4 %all-to-all-start.1 = ((f32[8,64,128]{2,1,0:T(8,128)}), f32[8,64,128]{2,1,0:T(8,128)S(1)}, u32[]{:S(2)}, u32[]{:S(2)}) async-start(f32[8,64,128]{2,1,0:T(8,128)} %get-tuple-element.12), calls=%async_computation.1 | async-start | bytes 524288 | tf_op jit(solution)/shard_map/all_to_all | solution.py:221
  77.0 33.0 %all-to-all-start = ((bf16[8,64,2304]{2,1,0:T(8,128)(2,1)}), bf16[8,64,2304]{2,1,0:T(8,128)(2,1)S(1)}, u32[]{:S(2)}, u32[]{:S(2)}) async-start(bf16[8,64,2304]{2,1,0:T(8,128)(2,1)} %get-tuple-element.11), calls=%async_computation | async-start | bytes 4718592 | tf_op jit(solution)/shard_map/all_to_all | solution.py:220
  83.1 19.5 %copy-start.9 = (s32[2,8]{1,0:T(2,128)S(1)}, s32[2,8]{1,0:T(2,128)}, u32[]{:S(2)}) copy-start(s32[2,8]{1,0:T(2,128)} %param.37) | copy-start | bytes 196
  110.0 1.1 copy-start.3
  111.0 1.0 copy-start.4
  112.0 0.8 copy-start.5
  162.4 1.7 copy-start.2
  217.2 2.0 copy-start.1
Sparse Core Ops, SparseCore 0:
  10.0 32.2 all-gather.4

commit v3 on v2

--- a/solution.py
+++ b/solution.py
@@ -89,41 +89,78 @@
     stat_ref[0] = stat
 
 
-def prompt_kernel(q_ref, group_ref, k_ref, v_ref, acc_ref, stat_ref):
-    g = pl.program_id(0)
-    sources, rows = q_ref.shape[0], q_ref.shape[1]
+def prompt_kernel(
+    size, plane_ref, k_ref, v_ref, acc_ref, stat_ref, residual_ref, gain_ref,
+    att_ref, stream_ref, normed_ref,
+    k_wide, v_wide, staged, sstat, landed, lstat, asend, arecv, ssend, srecv,
+):
+    me = lax.axis_index("exp")
+    rows, width = acc_ref.shape
     groups, positions = k_ref.shape[0], k_ref.shape[1]
-    keys = groups * positions
-    k = k_ref[...].reshape(keys, LANES)
-    v = v_ref[...].reshape(keys, LANES)
+    keys, packs = groups * positions, width // LANES
     masks = head_masks(keys)
-    k_wide = jnp.concatenate([k * mask for mask in masks], axis=0)
-    v_wide = jnp.concatenate([v * mask for mask in masks], axis=0)
+    greet((("exp", size),))
+
+    def columns(g):
+        return pl.ds(pl.multiple_of(g * LANES, LANES), LANES)
+
+    def widen(g, carry):
+        k = k_ref[:, :, columns(g)].reshape(keys, LANES)
+        v = v_ref[:, :, columns(g)].reshape(keys, LANES)
+        for h in range(PACK):
+            k_wide[g, h * keys : (h + 1) * keys] = k * masks[h]
+            v_wide[g, h * keys : (h + 1) * keys] = v * masks[h]
+        return carry
+
+    lax.fori_loop(0, packs, widen, 0)
     key_group = (lax.broadcasted_iota(jnp.int32, (rows, keys), 1) // positions).astype(jnp.float32)
     lane = lax.broadcasted_iota(jnp.int32, (rows, STAT), 1)
-
-    @pl.when(g == 0)
-    def _():
-        stat_ref[...] = jnp.zeros_like(stat_ref)
-
-    for s in range(sources):
-        scores = lax.dot_general(q_ref[s], k_wide, NT, preferred_element_type=jnp.float32) * SCALE
-        live = key_group == group_ref[s].astype(jnp.float32)[:, :1]
-        stat = stat_ref[s]
-        weights = []
-        for h in range(PACK):
-            part = jnp.where(live, scores[:, h * keys : (h + 1) * keys], -jnp.inf)
-            top = jnp.max(part, axis=1, keepdims=True)
-            weight = jnp.exp(part - top)
-            stat = jnp.where(lane == g * PACK + h, top, stat)
-            stat = jnp.where(
-                lane == STAT // 2 + g * PACK + h, jnp.sum(weight, axis=1, keepdims=True), stat
-            )
-            weights.append(weight.astype(jnp.bfloat16))
-        stat_ref[s] = stat
-        acc_ref[s] = jnp.dot(
-            jnp.concatenate(weights, axis=1), v_wide, preferred_element_type=jnp.float32
-        ).astype(jnp.bfloat16)
+    copies = []
+    for o in list(range(1, size)) + [0]:
+        source = lax.rem(me + o, size)
+        live = key_group == plane_ref[source, :, width : width + STAT].astype(jnp.float32)[:, :1]
+        target, tstat = (staged.at[o - 1], sstat.at[o - 1]) if o else (landed.at[me], lstat.at[me])
+
+        def attend(g, stat):
+            scores = lax.dot_general(
+                plane_ref[source, :, columns(g)], k_wide[g], NT,
+                preferred_element_type=jnp.float32,
+            ) * SCALE
+            weights = []
+            for h in range(PACK):
+                part = jnp.where(live, scores[:, h * keys : (h + 1) * keys], -jnp.inf)
+                top = jnp.max(part, axis=1, keepdims=True)
+                weight = jnp.exp(part - top)
+                total = jnp.sum(weight, axis=1, keepdims=True)
+                stat = jnp.where(lane == g * PACK + h, top, stat)
+                stat = jnp.where(lane == STAT // 2 + g * PACK + h, total, stat)
+                weights.append(weight.astype(jnp.bfloat16))
+            target[:, columns(g)] = jnp.dot(
+                jnp.concatenate(weights, axis=1), v_wide[g], preferred_element_type=jnp.float32
+            ).astype(jnp.bfloat16)
+            return stat
+
+        tstat[...] = lax.fori_loop(0, packs, attend, jnp.zeros((rows, STAT), jnp.float32))
+        if o:
+            for copy in (
+                remote(target, landed.at[me], asend.at[o - 1], arecv.at[o - 1], "exp", source),
+                remote(tstat, lstat.at[me], ssend.at[o - 1], srecv.at[o - 1], "exp", source),
+            ):
+                copy.start()
+                copies.append(copy)
+    for copy in copies:
+        copy.wait_send()
+    for o in range(1, size):
+        origin = lax.rem(me - o + size, size)
+        remote(
+            staged.at[o - 1], landed.at[origin], asend.at[o - 1], arecv.at[o - 1], "exp", origin
+        ).wait_recv()
+        remote(
+            sstat.at[o - 1], lstat.at[origin], ssend.at[o - 1], srecv.at[o - 1], "exp", origin
+        ).wait_recv()
+    merge_kernel(
+        landed, lstat, acc_ref, stat_ref, residual_ref, gain_ref, att_ref, stream_ref, normed_ref
+    )
 
 
 def merge_kernel(
@@ -197,35 +234,29 @@
         ),
         name="local_attention",
     )(cache_lengths, queries, cache_keys, cache_values, draft_keys, draft_values, anc)
-    pblock = pl.BlockSpec((groups, positions, LANES), lambda g: (0, 0, g))
-    part, pstat = pl.pallas_call(
-        prompt_kernel,
-        grid=(packs,),
-        in_specs=[
-            pl.BlockSpec((sources, rows, LANES), lambda g: (0, 0, g)),
-            pl.BlockSpec((sources, rows, STAT), lambda g: (0, 0, width // STAT)),
-            pblock,
-            pblock,
+    keys = groups * positions
+    vmem = pl.BlockSpec(memory_space=pltpu.VMEM)
+    dma = pltpu.SemaphoreType.DMA
+    return pl.pallas_call(
+        functools.partial(prompt_kernel, sources),
+        out_shape=[jax.ShapeDtypeStruct((rows, width), jnp.bfloat16)] * 3,
+        in_specs=[vmem] * 7,
+        out_specs=[vmem] * 3,
+        scratch_shapes=[
+            pltpu.VMEM((packs, PACK * keys, LANES), jnp.bfloat16),
+            pltpu.VMEM((packs, PACK * keys, LANES), jnp.bfloat16),
+            pltpu.VMEM((sources - 1, rows, width), jnp.bfloat16),
+            pltpu.VMEM((sources - 1, rows, STAT), jnp.float32),
+            pltpu.VMEM((sources, rows, width), jnp.bfloat16),
+            pltpu.VMEM((sources, rows, STAT), jnp.float32),
+            dma((sources - 1,)), dma((sources - 1,)), dma((sources - 1,)), dma((sources - 1,)),
         ],
-        out_specs=[
-            pl.BlockSpec((sources, rows, LANES), lambda g: (0, 0, g)),
-            pl.BlockSpec((sources, rows, STAT), lambda g: (0, 0, 0)),
-        ],
-        out_shape=[
-            jax.ShapeDtypeStruct((sources, rows, width), jnp.bfloat16),
-            jax.ShapeDtypeStruct((sources, rows, STAT), jnp.float32),
-        ],
+        compiler_params=pltpu.CompilerParams(
+            collective_id=2, has_side_effects=True, vmem_limit_bytes=48 * 1024 * 1024
+        ),
         name="prompt_attention",
-    )(plane, plane, prompt_keys, prompt_values)
-    part = lax.all_to_all(part, "exp", split_axis=0, concat_axis=0, tiled=True)
-    pstat = lax.all_to_all(pstat, "exp", split_axis=0, concat_axis=0, tiled=True)
-    return pl.pallas_call(
-        merge_kernel,
-        out_shape=[jax.ShapeDtypeStruct((rows, width), jnp.bfloat16)] * 3,
-        compiler_params=pltpu.CompilerParams(vmem_limit_bytes=32 * 1024 * 1024),
-        name="merge",
     )(
-        part, pstat, acc.reshape(rows, width), stat.reshape(rows, STAT),
+        plane, prompt_keys, prompt_values, acc.reshape(rows, width), stat.reshape(rows, STAT),
         residual.reshape(rows, width), norm_gain.reshape(1, width),
     )
 
@@ -250,7 +281,7 @@
 
 
 def dispatch_kernel(
-    depth, size, rows_ref, pick_ref, out_ref, held, staged, zsend, zrecv, psend, precv, own
+    depth, size, rows_ref, pick_ref, router_ref, out_ref, logits_ref, held, staged, zsend, zrecv, psend, precv, own
 ):
     z, e = lax.axis_index("req"), lax.axis_index("exp")
     experts, cap = pick_ref.shape[1], pick_ref.shape[2]
@@ -274,6 +305,7 @@
             staged[k, x] = jnp.dot(
                 pick_ref[source, x], rows, preferred_element_type=jnp.float32
             ).astype(jnp.bfloat16)
+        logits_ref[source] = jnp.dot(rows, router_ref[...], preferred_element_type=jnp.float32)
         for o in range(1, size):
             target = lax.rem(e + o, size)
             copy = remote(
@@ -359,16 +391,19 @@
             copy.wait_send()
 
 
-def dispatch(normed, pick, depth, size):
+def dispatch(normed, pick, router, depth, size):
     rows, width = normed.shape
     cap = pick.shape[2]
     dma = pltpu.SemaphoreType.DMA
     vmem = pl.BlockSpec(memory_space=pltpu.VMEM)
     return pl.pallas_call(
         functools.partial(dispatch_kernel, depth, size),
-        out_shape=jax.ShapeDtypeStruct((depth, size, cap, width), jnp.bfloat16),
-        in_specs=[vmem, vmem],
-        out_specs=pl.BlockSpec(memory_space=pl.ANY),
+        out_shape=[
+            jax.ShapeDtypeStruct((depth, size, cap, width), jnp.bfloat16),
+            jax.ShapeDtypeStruct((depth, rows, STAT), jnp.float32),
+        ],
+        in_specs=[vmem, vmem, vmem],
+        out_specs=[pl.BlockSpec(memory_space=pl.ANY), vmem],
         scratch_shapes=[
             pltpu.VMEM((depth - 1, rows, width), jnp.bfloat16),
             pltpu.VMEM((depth, pick.shape[1], cap, width), jnp.bfloat16),
@@ -379,7 +414,7 @@
             collective_id=0, has_side_effects=True, vmem_limit_bytes=40 * 1024 * 1024
         ),
         name="dispatch",
-    )(normed, pick)
+    )(normed, pick, router)
 
 
 def collect(y, mix, stream, depth, size):
@@ -433,26 +468,27 @@
         prompt_keys, prompt_values, group_ids, residual, norm_gain,
     )
     attended = attended.reshape(requests, tree_len, width)
-    logits = jnp.dot(normed, router, preferred_element_type=jnp.float32)
     routed = expert_ids.reshape(row_count, TOPK)
-    chosen = jnp.take_along_axis(logits, routed, axis=1)
-    gate_first = 1.0 / (1.0 + jnp.exp(chosen[:, 1] - chosen[:, 0]))
-    gates = jnp.stack([gate_first, 1.0 - gate_first], axis=1)
     depth, size = lax.axis_size("req"), lax.axis_size("exp")
     all_routed = lax.all_gather(routed, "req", axis=0, tiled=False)
-    all_gates = lax.all_gather(gates, "req", axis=0, tiled=False)
     target = all_routed * CAP + jax.vmap(slot_numbers)(all_routed)
     slots = jnp.arange(EXPERTS * CAP, dtype=jnp.int32).reshape(EXPERTS, CAP)
     pick = (target[:, None, None, :, 0] == slots[None, :, :, None]) | (
         target[:, None, None, :, 1] == slots[None, :, :, None]
     )
     pick = pick.astype(jnp.bfloat16)
+    arrived, logits = dispatch(
+        normed, pick, jnp.pad(router, ((0, 0), (0, STAT - EXPERTS))), depth, size
+    )
+    named = all_routed[..., None] == jnp.arange(EXPERTS, dtype=jnp.int32)
+    chosen = jnp.sum(jnp.where(named, logits[:, :, None, :EXPERTS], 0.0), axis=-1)
+    gate_first = 1.0 / (1.0 + jnp.exp(chosen[..., 1] - chosen[..., 0]))
+    all_gates = jnp.stack([gate_first, 1.0 - gate_first], axis=-1)
     hit = target[:, None, :, None, :] == slots[None, :, None, :, None]
     mix = jnp.sum(jnp.where(hit, all_gates[:, None, :, None, :], 0.0), axis=-1)
     mix_high = mix.astype(jnp.bfloat16)
     mix_low = (mix - lax.reduce_precision(mix, 8, 7)).astype(jnp.bfloat16)
     mix = jnp.concatenate([mix_high, mix_low], axis=2)
-    arrived = dispatch(normed, pick, depth, size)
     row_piece = arrived.reshape(-1, width)
     gate_proj = jnp.dot(row_piece, w_gate[0], preferred_element_type=jnp.float32)
     up_proj = jnp.dot(row_piece, w_up[0], preferred_element_type=jnp.float32)

time: 273 us -> 252 us (0.923)
  waiting for transfers between devices: 28.7 us -> 0.02 us
  Pallas kernels: 139 us -> 163 us
  blocking collectives: 28 us -> 12.6 us
  starting transfers between devices: 7.21 us -> 0.04 us
  local copies, waits for them, and re-layouts: 21.6 us -> 25.6 us
  other arithmetic: 5.05 us -> 7.84 us
    all_gather x1, waiting for transfers between devices: 16.1 us -> 0.01 us  [attention(): plane = lax.all_gather(sent, 'exp', axis=0, tiled=False)]
    all_gather x1 -> x0, blocking collectives: 15.4 us -> none  [on_device(): all_gates = lax.all_gather(gates, 'req', axis=0, tiled=False)]
    pallas_call x2 -> x1, Pallas kernels: 30 us -> 43.2 us  [attention(): pl.pallas_call(functools.partial(prompt_kernel, sources), out_shape=[jax....]
    all_to_all x2 -> x0, waiting for transfers between devices: 12.5 us -> none  [the longest x1 6.42 us: attention(): part = lax.all_to_all(part, 'exp', split_axis=0, concat_axis=0, tiled=True)]
    all_to_all x2 -> x0, starting transfers between devices: 7.17 us -> none  [the longest x1 3.62 us: attention(): part = lax.all_to_all(part, 'exp', split_axis=0, concat_axis=0, tiled=True)]
    pallas_call x1, Pallas kernels: 43.8 us -> 49.5 us  [dispatch(): pl.pallas_call(functools.partial(dispatch_kernel, depth, size), out_shape...]
    pallas_call x1, Pallas kernels: 45.3 us -> 50.7 us  [collect(): pl.pallas_call(functools.partial(collect_kernel, depth, size), out_shape=...]
    unnamed x22 -> x42, local copies, waits for them, and re-layouts: 7.95 us -> 10.9 us
  transfers between devices with their start and end apart: 3 -> 1, of which waited for: 3 -> 0; matrix products, arithmetic and copies ran while one was open for 3% -> 5% of each run, Pallas kernels for 7% -> 8%
where the time goes in v3:
time: 252 us; the launch traced here: 250 us
  Pallas kernels  163 us (65%)
  matrix products  27.2 us (11%)
  local copies, waits for them, and re-layouts  25.6 us (10%)
  between operations  14.3 us (6%)
  blocking collectives  12.6 us (5%)
  other arithmetic  7.84 us (3%)
    pallas_call x1, Pallas kernels, collect(): pl.pallas_call(functools.partial(collect_kernel, depth, size), out_shape=...  50.7 us
    pallas_call x1, Pallas kernels, dispatch(): pl.pallas_call(functools.partial(dispatch_kernel, depth, size), out_shape...  49.5 us
    pallas_call x1, Pallas kernels, attention(): pl.pallas_call(functools.partial(prompt_kernel, sources), out_shape=[jax....  43.2 us
    pallas_call x1, Pallas kernels, attention(): pl.pallas_call(local_kernel, grid_spec=pltpu.PrefetchScalarGridSpec(num_s...  19.5 us
    dot_general x1, matrix products, on_device(): jnp.dot(hidden, w_down[0], preferred_element_type=jnp.float32)  15.9 us
    all_gather x1, blocking collectives, on_device(): all_routed = lax.all_gather(routed, 'req', axis=0, tiled=False)  12.6 us
    unnamed x42, local copies, waits for them, and re-layouts  10.9 us
    dot_general x1, matrix products, on_device(): jnp.dot(row_piece, w_gate[0], preferred_element_type=jnp.float32)  9.88 us
  transfers between devices with their start and end apart: 1, of which 0 were waited for; matrix products, arithmetic and copies ran while one was open for 5% of the time, Pallas kernels for 8%

profile of v3, /device:TPU:0, one launch (start us, length us, event | category | flops | bytes accessed | tf_op | source)
XLA Modules:
  0.0 250.5 jit_solution(5613883905666375263)
XLA Ops:
  8.2 1.7 pad_maximum_fusion
  11.4 12.6 %all_gather.11 = s32[4,64,2]{1,2,0:T(2,128)S(1)} all-gather(s32[1,64,2]{1,2,0:T(2,128)S(1)} %all_gather_reshape.3), channel_id=1, replica_groups=mesh['req'=4,'exp'=8] {'req'}, dimensions={0}, use_global_device_ids=true | all-gather | bytes 2560 | tf_op jit(solution)/shard_map/all_gather | solution.py:473
  25.0 1.1 copy.80
  28.2 1.8 gather_fusion
  30.0 0.8 gather_fusion.1
  30.8 0.9 pad.4.router_ref
  33.2 19.5 %local_attention.1 = (f32[2,32,2304]{2,1,0:T(8,128)}, f32[2,32,128]{2,1,0:T(8,128)}) custom-call(s32[2]{0:T(128)} %len_ref.1, bf16[2,32,2304]{2,1,0:T(8,128)(2,1)} %q_ref.1, bf16[2,768,2304]{2,1,0:T(8,128)(2,1)} %kc_ref.1, bf16[2,768,2304]{2,1,0:T(8,128)(2,1)} %vc_ref.1, bf16[2,32,2304]{2,1,0:T(8,128)(2,1)} %kd_ref.1, bf16[2,32,2304]{2,1,0:T(8,128)(2,1)} %vd_ref.1, ...), custom_call_target="tpu_custom_call" | custom-call | flops 1887436800 | bytes 14155776 | tf_op jit(solution)/shard_map/local_attention/pallas_call | solution.py:216
  52.8 0.8 or_convert_fusion.pick_ref
  54.4 1.7 copy-done.1
  56.0 1.1 copy-done.6
  57.9 43.2 %prompt_attention.1 = (bf16[64,2304]{1,0:T(8,128)(2,1)S(1)}, bf16[64,2304]{1,0:T(8,128)(2,1)S(1)}, bf16[64,2304]{1,0:T(8,128)(2,1)S(1)}) custom-call(bf16[8,64,2432]{2,1,0:T(8,128)(2,1)S(1)} %bitcast.64, bf16[2,64,2304]{2,1,0:T(8,128)(2,1)S(1)} %copy-done.4, bf16[2,64,2304]{2,1,0:T(8,128)(2,1)S(1)} %copy-done.5, f32[64,2304]{1,0:T(8,128)S(1)} %bitcast.66, ...), custom_call_target="tpu_custom_call" | custom-call | tf_op jit(solution)/shard_map/prompt_attention/pallas_call | solution.py:240
  101.1 1.3 copy-done.2
  102.4 49.5 %dispatch.1 = (bf16[4,8,18,2304]{3,2,1,0:T(8,128)(2,1)S(1)}, f32[4,64,128]{2,1,0:T(8,128)S(1)}) custom-call(bf16[64,2304]{1,0:T(8,128)(2,1)S(1)} %get-tuple-element.14.rows_ref, bf16[4,8,18,64]{3,2,1,0:T(8,128)(2,1)S(1)} %copy-done.3, bf16[2304,128]{1,0:T(8,128)(2,1)S(1)} %copy-done.2), custom_call_target="tpu_custom_call" | custom-call | tf_op jit(solution)/shard_map/dispatch/pallas_call | solution.py:399
  152.5 2.4 reshape.92
  154.9 9.9 %fusion.4 = f32[576,1440]{1,0:T(8,128)} fusion(bf16[576,2304]{1,0:T(8,128)(2,1)} %reshape.92, bf16[1,2304,1440]{1,2,0:T(8,128)(2,1)} %param.33), kind=kOutput, calls=%fused_computation.6 | convolution fusion | flops 3822059520 | bytes 12607488 | tf_op jit(solution)/shard_map/dot_general | solution.py:493
  164.8 15.9 %fusion.6 = bf16[576,2304]{1,0:T(8,128)(2,1)} fusion(bf16[1,1440,2304]{2,1,0:T(8,128)(2,1)} %param.35, f32[576,1440]{1,0:T(8,128)} %fusion.4, bf16[576,2304]{1,0:T(8,128)(2,1)S(1)} %copy-done.14, bf16[1,2304,1440]{1,2,0:T(8,128)(2,1)} %param.34), kind=kOutput, calls=%fused_computation.8 | convolution fusion | flops 7650422784 | bytes 21897216 | tf_op jit(solution)/shard_map/dot_general | solution.py:496
  180.7 2.8 %reshape.93.y_ref = bf16[4,8,18,2304]{3,2,1,0:T(8,128)(2,1)S(1)} reshape(bf16[576,2304]{1,0:T(8,128)(2,1)} %fusion.6) | data formatting | bytes 5308416 | tf_op jit(solution)/shard_map/reshape | solution.py:498
  183.5 1.0 copy.83
  185.3 0.9 select_reduce_fusion
  186.2 0.8 pad_maximum_fusion.1
  187.0 2.3 copy.84.mix_ref
  189.3 1.2 copy-done
  190.5 1.0 copy-done.9
  191.5 50.7 %collect.1 = bf16[64,2304]{1,0:T(8,128)(2,1)S(1)} custom-call(bf16[4,8,18,2304]{3,2,1,0:T(8,128)(2,1)S(1)} %reshape.93.y_ref, bf16[4,8,128,18]{3,2,1,0:T(8,128)(2,1)S(1)} %copy-done, bf16[64,2304]{1,0:T(8,128)(2,1)S(1)} %copy-done.9), custom_call_target="tpu_custom_call" | custom-call | tf_op jit(solution)/shard_map/collect/pallas_call | solution.py:425
  (76 shorter events, 11.5 us)
Async XLA Ops:
  7.2 22.8 %copy-start.15 = (bf16[2,32,2304]{2,1,0:T(8,128)(2,1)S(1)}, bf16[2,32,2304]{2,1,0:T(8,128)(2,1)}, u32[]{:S(2)}) copy-start(bf16[2,32,2304]{2,1,0:T(8,128)(2,1)} %vd_ref.1) | copy-start | bytes 884740
  7.2 24.6 %copy-start.18 = (s32[2,32]{1,0:T(2,128)S(1)}, s32[2,32]{1,0:T(2,128)}, u32[]{:S(2)}) copy-start(s32[2,32]{1,0:T(2,128)} %param.23) | copy-start | bytes 772
  7.2 47.1 %all-gather.3.cloned.1.call-start = ((), (), s32[]{:S(2)}) async-start(), calls=%async_computation | async-start | bytes 2801664 | tf_op jit(solution)/shard_map/all_gather | solution.py:211
  24.0 3.5 %copy-start.16 = (s32[4,64,2]{1,2,0:T(2,128)}, s32[4,64,2]{1,2,0:T(2,128)S(1)}, u32[]{:S(2)}) copy-start(s32[4,64,2]{1,2,0:T(2,128)S(1)} %all_gather.11) | copy-start | bytes 6148
  33.2 19.5 %copy-start.17 = (s32[2,8]{1,0:T(2,128)S(1)}, s32[2,8]{1,0:T(2,128)}, u32[]{:S(2)}) copy-start(s32[2,8]{1,0:T(2,128)} %param.37) | copy-start | bytes 196
  33.2 21.1 %copy-start.4 = (bf16[2,64,2304]{2,1,0:T(8,128)(2,1)S(1)}, bf16[2,64,2304]{2,1,0:T(8,128)(2,1)}, u32[]{:S(2)}) copy-start(bf16[2,64,2304]{2,1,0:T(8,128)(2,1)} %k_ref.1) | copy-start | bytes 1769476
  33.2 21.1 %copy-start.5 = (bf16[2,64,2304]{2,1,0:T(8,128)(2,1)S(1)}, bf16[2,64,2304]{2,1,0:T(8,128)(2,1)}, u32[]{:S(2)}) copy-start(bf16[2,64,2304]{2,1,0:T(8,128)(2,1)} %v_ref.1) | copy-start | bytes 1769476
  33.2 21.1 %copy-start.7 = (bf16[2,32,2304]{2,1,0:T(8,128)(2,1)S(1)}, bf16[2,32,2304]{2,1,0:T(8,128)(2,1)}, u32[]{:S(2)}) copy-start(bf16[2,32,2304]{2,1,0:T(8,128)(2,1)} %param.30) | copy-start | bytes 884740
  54.3 1.7 copy-start.1
  56.0 1.1 copy-start.6
  57.1 0.8 copy-start.13
  57.9 43.3 %copy-start.3 = (bf16[4,8,18,64]{3,2,1,0:T(8,128)(2,1)S(1)}, bf16[4,8,18,64]{3,2,1,0:T(8,128)(2,1)}, u32[]{:S(2)}) copy-start(bf16[4,8,18,64]{3,2,1,0:T(8,128)(2,1)} %or_convert_fusion.pick_ref) | copy-start | bytes 221188
  101.1 50.8 %copy-start.8 = (bf16[64,2304]{1,0:T(8,128)(2,1)}, bf16[64,2304]{1,0:T(8,128)(2,1)S(1)}, u32[]{:S(2)}) copy-start(bf16[64,2304]{1,0:T(8,128)(2,1)S(1)} %get-tuple-element.17.stream_ref) | copy-start | bytes 884740
  101.1 50.8 %copy-start.10 = (bf16[64,2304]{1,0:T(8,128)(2,1)}, bf16[64,2304]{1,0:T(8,128)(2,1)S(1)}, u32[]{:S(2)}) copy-start(bf16[64,2304]{1,0:T(8,128)(2,1)S(1)} %get-tuple-element.13) | copy-start | bytes 884740
  101.1 1.3 copy-start.2
  151.9 0.6 copy-start.12
  154.9 9.9 %copy-start.14 = (bf16[576,2304]{1,0:T(8,128)(2,1)S(1)}, bf16[576,2304]{1,0:T(8,128)(2,1)}, u32[]{:S(2)}) copy-start(bf16[576,2304]{1,0:T(8,128)(2,1)} %reshape.92) | copy-start | bytes 7962628
  189.3 1.2 copy-start
  190.5 1.0 copy-start.9
  191.5 50.7 %copy-start.11 = (bf16[64,2304]{1,0:T(8,128)(2,1)S(1)}, bf16[64,2304]{1,0:T(8,128)(2,1)}, u32[]{:S(2)}) copy-start(bf16[64,2304]{1,0:T(8,128)(2,1)} %copy-done.10) | copy-start | bytes 884740
Sparse Core Ops, SparseCore 0:
  10.0 32.3 all-gather.2
